TPU v7x, 512 devices: a whole 4x8x8 slice. The times are simulated.
512 devices in a mesh: freq: 16 (over y, core), offset: 32 (over x, z).
Axes of the slice: x: 4, y: 8, z: 8, core: 2. Of those that a mesh axis runs over, the one named last changes fastest.
Arguments:
- raw_traces: bfloat16 [32768, 2048], P('offset', 'freq'), may hold values from -6 to 6
- trace_slot: int32 [32, 1024], P(None, 'offset'), may hold values from 0 to 1023, as said below
- offset_index: int32 [1024], replicated, may hold values from 1 to 1023
- slowness_index: int32 [256], replicated, may hold values from 0 to 511
Outputs:
- radon: float32 [256, 1024, 64], P('offset', 'freq')
Inputs may be any that keep to these rules, and one draw needn't show every extreme that they name: `trace_slot`: in every aligned block of 32 columns, the 32 x 32 entries name each of 0 to 1023 exactly once.
All inputs are finite; a program needn't handle non-finite values.
Results may differ from a plain program's by a relative error of at most 0.0046.
Values may be sent and summed in bfloat16 or wider, within the bound.
A program may use at most 64 MiB of HBM per device.

v0:
```python
import math

import jax
import jax.numpy as jnp
from jax import lax
from jax.sharding import Mesh
from jax.sharding import PartitionSpec as P

NF = 1024
OFFSET = ("offset_0", "offset_1")


APEX_TIME = 100.0
CURVATURE = 0.0003


def own_rows(total, axes):
    for axis in axes:
        total = lax.psum_scatter(total, axis, scatter_dimension=0, tiled=True)
    return total


def moveout(slowness, offset_grid):
    spread = (
        CURVATURE * slowness.astype(jnp.float32)[:, None] * offset_grid.astype(jnp.float32)[None, :]
    )
    return jnp.sqrt(APEX_TIME * APEX_TIME + spread * spread) - APEX_TIME


def whole_table(local_freqs, total_time):
    column_total = 2 * NF
    column = jnp.arange(column_total, dtype=jnp.int32)
    band_ids = column // (2 * local_freqs)
    within = column % (2 * local_freqs)
    freq_ids = band_ids * local_freqs + within % local_freqs
    shifts = jnp.where(within < local_freqs, 0, total_time // 2).astype(jnp.int32)
    odd_rates = 2 * freq_ids + 1
    fine_size = 64
    coarse_size = total_time // fine_size
    period = 2 * total_time
    coarse_ids = jnp.arange(coarse_size, dtype=jnp.int32)[:, None]
    fine_ids = jnp.arange(fine_size, dtype=jnp.int32)[:, None]
    coarse_turn = coarse_ids * fine_size % period * odd_rates[None, :] % period
    fine_turn = (fine_ids * odd_rates[None, :] + shifts[None, :]) % period
    coarse_angle = coarse_turn.astype(jnp.float32) * (math.pi / total_time)
    fine_angle = fine_turn.astype(jnp.float32) * (math.pi / total_time)
    coarse_cos = jnp.cos(coarse_angle)
    coarse_sin = jnp.sin(coarse_angle)
    fine_cos = jnp.cos(fine_angle)
    fine_sin = jnp.sin(fine_angle)
    values = (
        coarse_cos[:, None, :] * fine_cos[None, :, :]
        - coarse_sin[:, None, :] * fine_sin[None, :, :]
    )
    values = values.reshape(total_time, column_total)
    return (values * (1.0 / math.sqrt(total_time))).astype(jnp.bfloat16)


def local(raw_traces, trace_slot, offset_index, slowness_index):
    gathers, local_offsets = trace_slot.shape
    local_times = raw_traces.shape[1]
    freq_devices = lax.axis_size("freq")
    offset_devices = lax.axis_size(OFFSET)
    total_time = local_times * freq_devices
    local_freqs = NF // freq_devices
    trace_rows = gathers * local_offsets
    picked = raw_traces[trace_slot.reshape(-1)]
    grouped = picked.reshape(freq_devices, trace_rows // freq_devices, local_times)
    fourier_table = whole_table(local_freqs, total_time)
    series = lax.all_to_all(grouped, "freq", split_axis=0, concat_axis=2, tiled=True)
    flattened = series.reshape(series.shape[1], total_time)
    spectrum = jnp.dot(flattened, fourier_table, preferred_element_type=jnp.float32).astype(
        jnp.bfloat16
    )
    spectrum = jnp.transpose(
        spectrum.reshape(flattened.shape[0], freq_devices, 2 * local_freqs), (1, 0, 2)
    )
    assembled = lax.all_to_all(spectrum, "freq", split_axis=0, concat_axis=0, tiled=True)
    spectra = assembled.reshape(gathers, local_offsets, 2 * local_freqs)
    real_part = spectra[:, :, :local_freqs]
    imag_part = spectra[:, :, local_freqs:]
    freq_ids = lax.axis_index("freq") * local_freqs + jnp.arange(local_freqs, dtype=jnp.int32)
    angular = (2 * freq_ids + 1).astype(jnp.float32) * (math.pi / total_time)
    own_offsets = lax.dynamic_slice_in_dim(
        offset_index, lax.axis_index(OFFSET) * local_offsets, local_offsets
    )
    delays = moveout(slowness_index, own_offsets)
    phases = angular[:, None, None] * delays[None, :, :]
    cosine = jnp.cos(phases).astype(jnp.bfloat16)
    sines = jnp.sin(phases).astype(jnp.bfloat16)
    real_out = jnp.einsum(
        "fph,ghf->pfg", cosine, real_part, preferred_element_type=jnp.float32
    ) - jnp.einsum("fph,ghf->pfg", sines, imag_part, preferred_element_type=jnp.float32)
    imag_out = jnp.einsum(
        "fph,ghf->pfg", sines, real_part, preferred_element_type=jnp.float32
    ) + jnp.einsum("fph,ghf->pfg", cosine, imag_part, preferred_element_type=jnp.float32)
    summed = own_rows(jnp.concatenate([real_out, imag_out], axis=2), OFFSET)
    return summed * (1.0 / math.sqrt(local_offsets * offset_devices))


def solution(mesh):
    torus = Mesh(mesh.devices.reshape(mesh.shape["freq"], 4, 8), ("freq", "offset_0", "offset_1"))
    placed = (P(OFFSET, "freq"), P(None, OFFSET), P(), P())
    return jax.shard_map(
        local, mesh=torus, in_specs=placed, out_specs=P(OFFSET, "freq", None), check_vma=False
    )
```

profile of v0, /device:TPU:1, one launch (start us, length us, event | category | flops | bytes accessed | tf_op | source)
XLA Modules:
  0.0 203.0 jit_solution(16207781302193923566)
XLA Ops:
  6.5 0.0 copy-start
  6.5 0.8 reshape.308
  7.4 0.1 copy-done
  7.5 4.3 %gather_fusion = bf16[1024,128]{1,0:T(8,128)(2,1)} fusion(bf16[1024,128]{1,0:T(8,128)(2,1)S(1)} %copy-done, s32[1024]{0:T(1024)S(1)} %broadcast_clamp_fusion), kind=kCustom, calls=%fused_computation | custom fusion | bytes 528384 | tf_op jit(solution)/shard_map/gather | solution.py:67
  11.8 10.2 %all-to-all-start = ((bf16[16,64,128]{2,1,0:T(8,128)(2,1)}), bf16[16,64,128]{2,1,0:T(8,128)(2,1)S(1)}, u32[]{:S(2)}, u32[]{:S(2)}) async-start(bf16[16,64,128]{2,1,0:T(8,128)(2,1)} %bitcast.1), calls=%async_computation | async-start | bytes 524288 | tf_op jit(solution)/shard_map/all_to_all | solution.py:70
  22.0 2.1 %fusion.21 = (f32[64,2048]{1,0:T(8,128)S(1)}, f32[64,2048]{1,0:T(8,128)S(1)}) fusion(s32[2048]{0:T(1024)S(1)} %get-tuple-element.12, s32[2048]{0:T(1024)S(1)} %get-tuple-element.11), kind=kLoop, calls=%fused_computation.33 | loop fusion | flops 1966080 | bytes 1064960 | tf_op jit(solution)/shard_map/cos | solution.py:49
  24.1 1.1 fusion.28
  25.2 6.2 %multiply_convert_fusion = bf16[32,64,2048]{2,1,0:T(8,128)(2,1)} fusion(f32[64,2048]{1,0:T(8,128)S(1)} %get-tuple-element.8, f32[32,2048]{1,0:T(8,128)S(1)} %get-tuple-element.10, f32[64,2048]{1,0:T(8,128)S(1)} %get-tuple-element.7, f32[32,2048]{1,0:T(8,128)S(1)} %get-tuple-element.9), kind=kLoop, calls=%fused_computation.1 | loop fusion | flops 20971520 | bytes 9961472 | tf_op jit(solution)/shard_map/convert_element_type | solution.py:56
  31.4 2.4 %all-to-all-done = bf16[16,64,128]{2,1,0:T(8,128)(2,1)S(1)} async-done(((bf16[16,64,128]{2,1,0:T(8,128)(2,1)}), bf16[16,64,128]{2,1,0:T(8,128)(2,1)S(1)}, u32[]{:S(2)}, u32[]{:S(2)}) %all-to-all-start) | async-done | bytes 262176 | tf_op jit(solution)/shard_map/all_to_all | solution.py:70
  33.7 0.2 copy.12
  33.9 0.0 copy-start.1
  33.9 5.0 %fusion.8 = bf16[8,16,8,128]{3,2,1,0:T(8,128)(2,1)S(1)} fusion(bf16[2048,2048]{1,0:T(8,128)(2,1)} %bitcast.32, bf16[8,8,16,128]{3,2,1,0:T(8,128)(2,1)S(1)} %bitcast.36), kind=kOutput, calls=%fused_computation.12 | convolution fusion | flops 537001984 | bytes 8912896 | tf_op jit(solution)/shard_map/dot_general | solution.py:72
  38.9 0.8 copy.30
  39.6 4.9 %all-to-all-start.1 = ((bf16[16,64,128]{2,1,0:T(8,128)(2,1)}), bf16[16,64,128]{2,1,0:T(8,128)(2,1)S(1)}, u32[]{:S(2)}, u32[]{:S(2)}) async-start(bf16[16,64,128]{2,1,0:T(8,128)(2,1)} %bitcast.31), calls=%async_computation.1 | async-start | bytes 524288 | tf_op jit(solution)/shard_map/all_to_all | solution.py:78
  44.5 0.2 reduce-scatter.7.cloned.1.call-start
  44.8 0.8 dynamic-slice_convert_fusion
  45.5 0.0 copy-done.1
  45.5 0.1 sqrt_add_fusion
  45.6 10.5 %all-to-all-done.1 = bf16[16,64,128]{2,1,0:T(8,128)(2,1)S(1)} async-done(((bf16[16,64,128]{2,1,0:T(8,128)(2,1)}), bf16[16,64,128]{2,1,0:T(8,128)(2,1)S(1)}, u32[]{:S(2)}, u32[]{:S(2)}) %all-to-all-start.1) | async-done | bytes 262176 | tf_op jit(solution)/shard_map/all_to_all | solution.py:78
  56.1 0.1 fusion.44
  56.3 0.8 copy.21
  57.1 8.5 %fusion.2 = f32[64,32,256]{2,1,0:T(8,128)} fusion(bf16[32,32,64]{1,0,2:T(8,128)(2,1)S(1)} %copy.21, f32[256,32]{0,1:T(8,128)S(1)} %sqrt_add_fusion, f32[64]{0:T(128)S(1)} %convert_multiply_fusion.1), kind=kOutput, calls=%fused_computation.10 | convolution fusion | flops 34603008 | bytes 2261248 | tf_op jit(solution)/shard_map/fph,ghf->pfg/dot_general | solution.py:94
  65.5 6.9 %fusion.6 = f32[64,32,256]{2,1,0:T(8,128)S(1)} fusion(bf16[32,32,64]{1,0,2:T(8,128)(2,1)S(1)} %copy.21, f32[256,32]{0,1:T(8,128)S(1)} %sqrt_add_fusion, f32[64]{0:T(128)S(1)} %convert_multiply_fusion.1), kind=kOutput, calls=%fused_computation.11 | convolution fusion | flops 34603008 | bytes 2261248 | tf_op jit(solution)/shard_map/fph,ghf->pfg/dot_general | solution.py:91
  72.4 0.8 copy.22
  73.2 9.6 %add_bitcast_fusion = f32[256,64,32]{0,2,1:T(8,128)S(1)} fusion(f32[64,32,256]{2,1,0:T(8,128)} %fusion.2, bf16[32,32,64]{1,0,2:T(8,128)(2,1)S(1)} %copy.22, f32[256,32]{0,1:T(8,128)S(1)} %sqrt_add_fusion, f32[64]{0:T(128)S(1)} %convert_multiply_fusion.1), kind=kOutput, calls=%fused_computation.8 | convolution fusion | flops 35127296 | bytes 4358400 | tf_op jit(solution)/shard_map/fph,ghf->pfg/dot_general | solution.py:96
  82.8 7.0 %subtract_bitcast_fusion = f32[256,64,32]{0,2,1:T(8,128)S(1)} fusion(f32[64,32,256]{2,1,0:T(8,128)S(1)} %fusion.6, bf16[32,32,64]{1,0,2:T(8,128)(2,1)S(1)} %copy.22, f32[256,32]{0,1:T(8,128)S(1)} %sqrt_add_fusion, f32[64]{0:T(128)S(1)} %convert_multiply_fusion.1), kind=kOutput, calls=%fused_computation.9 | convolution fusion | flops 35127296 | bytes 4358400 | tf_op jit(solution)/shard_map/fph,ghf->pfg/dot_general | solution.py:93
  89.8 2.2 %pad_maximum_fusion = f32[256,64,64]{0,2,1:T(8,128)} fusion(f32[256,64,32]{0,2,1:T(8,128)S(1)} %add_bitcast_fusion, f32[256,64,32]{0,2,1:T(8,128)S(1)} %subtract_bitcast_fusion), kind=kLoop, calls=%fused_computation.2 | loop fusion | flops 1048576 | bytes 8388608 | tf_op jit(solution)/shard_map/concatenate | solution.py:97
  92.1 5.6 %copy.19 = f32[256,4096]{1,0:T(8,128)} copy(f32[256,4096]{0,1:T(8,128)} %bitcast.33) | data formatting | bytes 8388608
  97.7 0.0 reduce-scatter.7.cloned.1.call-update
  97.7 0.0 reduce-scatter.5.cloned.1.call-start
  97.8 50.5 %reduce-scatter.7.cloned.1.call-done = f32[64,4096]{1,0:T(8,128)} async-done(((f32[256,4096]{1,0:T(8,128)}), f32[64,4096]{1,0:T(8,128)}) %reduce-scatter.7.cloned.1.call-update) | async-done | bytes 1048592
  148.2 1.8 copy.20
  150.1 2.7 %copy.16 = f32[64,64,64]{2,1,0:T(8,128)} copy(f32[64,64,64]{0,2,1:T(8,128)S(1)} %bitcast.34) | data formatting | bytes 2097152 | tf_op jit(solution)/shard_map/reduce_scatter | solution.py:19
  152.8 0.0 reduce-scatter.5.cloned.1.call-update
  152.8 41.7 %reduce-scatter.5.cloned.1.call-done = f32[8,64,64]{2,1,0:T(8,128)} async-done(((f32[64,64,64]{2,1,0:T(8,128)}), f32[8,64,64]{2,1,0:T(8,128)}) %reduce-scatter.5.cloned.1.call-update) | async-done | bytes 131088 | tf_op jit(solution)/shard_map/reduce_scatter | solution.py:19
  194.5 1.7 broadcast_multiply_fusion
  (6 shorter events, 0.0 us)
Async XLA Ops:
  6.5 1.0 copy-start
  11.8 21.9 %all-to-all-start = ((bf16[16,64,128]{2,1,0:T(8,128)(2,1)}), bf16[16,64,128]{2,1,0:T(8,128)(2,1)S(1)}, u32[]{:S(2)}, u32[]{:S(2)}) async-start(bf16[16,64,128]{2,1,0:T(8,128)(2,1)} %bitcast.1), calls=%async_computation | async-start | bytes 524288 | tf_op jit(solution)/shard_map/all_to_all | solution.py:70
  33.9 11.7 %copy-start.1 = (s32[256]{0:T(256)S(1)}, s32[256]{0:T(256)}, u32[]{:S(2)}) copy-start(s32[256]{0:T(256)} %param.7) | copy-start | bytes 3076
  39.6 16.5 %all-to-all-start.1 = ((bf16[16,64,128]{2,1,0:T(8,128)(2,1)}), bf16[16,64,128]{2,1,0:T(8,128)(2,1)S(1)}, u32[]{:S(2)}, u32[]{:S(2)}) async-start(bf16[16,64,128]{2,1,0:T(8,128)(2,1)} %bitcast.31), calls=%async_computation.1 | async-start | bytes 524288 | tf_op jit(solution)/shard_map/all_to_all | solution.py:78
  44.5 103.7 %reduce-scatter.7.cloned.1.call-start = ((), (), s32[]{:S(2)}) async-start(), calls=%async_computation.5 | async-start | bytes 5242880
  97.7 96.8 %reduce-scatter.5.cloned.1.call-start = ((), (), s32[]{:S(2)}) async-start(), calls=%async_computation.4 | async-start | bytes 2359296 | tf_op jit(solution)/shard_map/reduce_scatter | solution.py:19
Sparse Core Ops, SparseCore 0:
  97.8 50.3 reduce-scatter.6
  152.9 41.5 reduce-scatter.4
where the time goes:
time: 207 us; the launch traced here: 203 us
  waiting for transfers between devices  105 us (51%)
  matrix products  36.9 us (18%)
  local copies, waits for them, and re-layouts  18.1 us (9%)
  starting transfers between devices  15.3 us (7%)
  other arithmetic  14.1 us (7%)
  between operations  13.5 us (7%)
    unnamed x3, waiting for transfers between devices  50.5 us
    reduce_scatter x1, waiting for transfers between devices, own_rows(): total = lax.psum_scatter(total, axis, scatter_dimension=0, tiled=True)  41.7 us
    all_to_all x1, waiting for transfers between devices, local(): lax.all_to_all(spectrum, 'freq', split_axis=0, concat_axis=0, tiled=True)  10.5 us
    all_to_all x1, starting transfers between devices, local(): lax.all_to_all(grouped, 'freq', split_axis=0, concat_axis=2, tiled=True)  10.2 us
    dot_general x1, matrix products, local(): jnp.einsum('fph,ghf->pfg', cosine, imag_part, preferred_element_type=jnp....  9.6 us
    unnamed x8, local copies, waits for them, and re-layouts  9.12 us
    dot_general x1, matrix products, local(): jnp.einsum('fph,ghf->pfg', sines, real_part, preferred_element_type=jnp.f...  8.45 us
    dot_general x1, matrix products, local(): jnp.einsum('fph,ghf->pfg', sines, imag_part, preferred_element_type=jnp.f...  7.03 us
  transfers between devices with their start and end apart: 4, of which 4 were waited for; matrix products, arithmetic and copies ran while one was open for 5% of the time, Pallas kernels for 0%

commit v1 on v0

v1 whole, which is shorter than its diff:
```python
import math

import jax
import jax.numpy as jnp
from jax import lax
from jax.sharding import Mesh
from jax.sharding import PartitionSpec as P

NF = 1024
OFFSET = ("offset_0", "offset_1")
APEX_TIME = 100.0
CURVATURE = 0.0003


def moveout(slowness, offset_grid):
    spread = (
        CURVATURE * slowness.astype(jnp.float32)[:, None] * offset_grid.astype(jnp.float32)[None, :]
    )
    return jnp.sqrt(APEX_TIME * APEX_TIME + spread * spread) - APEX_TIME


def whole_table(total_time):
    column_total = 2 * NF
    column = jnp.arange(column_total, dtype=jnp.int32)
    freq_ids = column // 2
    shifts = jnp.where(column % 2 == 0, 0, total_time // 2).astype(jnp.int32)
    odd_rates = 2 * freq_ids + 1
    fine_size = 64
    coarse_size = total_time // fine_size
    period = 2 * total_time
    coarse_ids = jnp.arange(coarse_size, dtype=jnp.int32)[:, None]
    fine_ids = jnp.arange(fine_size, dtype=jnp.int32)[:, None]
    coarse_turn = coarse_ids * fine_size % period * odd_rates[None, :] % period
    fine_turn = (fine_ids * odd_rates[None, :] + shifts[None, :]) % period
    coarse_angle = coarse_turn.astype(jnp.float32) * (math.pi / total_time)
    fine_angle = fine_turn.astype(jnp.float32) * (math.pi / total_time)
    coarse_cos = jnp.cos(coarse_angle)
    coarse_sin = jnp.sin(coarse_angle)
    fine_cos = jnp.cos(fine_angle)
    fine_sin = jnp.sin(fine_angle)
    values = (
        coarse_cos[:, None, :] * fine_cos[None, :, :]
        - coarse_sin[:, None, :] * fine_sin[None, :, :]
    )
    values = values.reshape(total_time, column_total)
    return (values * (1.0 / math.sqrt(total_time))).astype(jnp.bfloat16)


def local(raw_traces, trace_slot, offset_index, slowness_index):
    gathers, local_offsets = trace_slot.shape
    local_times = raw_traces.shape[1]
    nk = lax.axis_size("freq")
    no = lax.axis_size(OFFSET)
    total_time = local_times * nk
    band = NF // nk
    pair = band // no
    hs = local_offsets // nk
    rows = hs * gathers
    picked = raw_traces[trace_slot.T.reshape(-1)]
    grouped = picked.reshape(nk, rows, local_times)
    table = whole_table(total_time)
    series = lax.all_to_all(grouped, "freq", split_axis=0, concat_axis=2, tiled=True)
    series = series.reshape(rows, total_time)
    spectrum = jnp.dot(series, table, preferred_element_type=jnp.float32).astype(jnp.bfloat16)
    c = 2 * pair
    spectrum = spectrum.reshape(hs, gathers, nk, no, c)
    spectrum = jnp.transpose(spectrum, (2, 3, 0, 4, 1)).reshape(nk, no, hs, c * gathers)
    first = lax.all_to_all(spectrum, "freq", split_axis=0, concat_axis=0, tiled=True)
    first = jnp.transpose(first, (1, 0, 2, 3)).reshape(no, nk * hs, c * gathers)
    second = lax.all_to_all(first, OFFSET, split_axis=0, concat_axis=0, tiled=True)
    spectra = second.reshape(no * nk * hs, c * gathers)

    freq_ids = lax.axis_index("freq") * band + lax.axis_index(OFFSET) * pair + jnp.arange(pair, dtype=jnp.int32)
    angular = (2 * freq_ids + 1).astype(jnp.float32) * (math.pi / total_time)
    delays = moveout(slowness_index, offset_index)
    phases = angular[:, None, None] * delays[None, :, :]
    cosine = jnp.cos(phases).astype(jnp.bfloat16)
    sines = jnp.sin(phases).astype(jnp.bfloat16)
    scale = 1.0 / math.sqrt(local_offsets * no)
    panels = []
    for f in range(pair):
        data = spectra[:, f * 2 * gathers:(f + 1) * 2 * gathers]
        cd = jnp.dot(cosine[f], data, preferred_element_type=jnp.float32)
        sd = jnp.dot(sines[f], data, preferred_element_type=jnp.float32)
        real_out = cd[:, :gathers] - sd[:, gathers:]
        imag_out = sd[:, :gathers] + cd[:, gathers:]
        panels.append(jnp.concatenate([real_out, imag_out], axis=1))
    panel = jnp.concatenate(panels, axis=1) * scale
    nps = panel.shape[0] // no
    panel = panel.reshape(no, nps, pair * 2 * gathers)
    got = lax.all_to_all(panel, OFFSET, split_axis=0, concat_axis=0, tiled=True)
    got = got.reshape(no, nps, pair, 2 * gathers)
    return jnp.transpose(got, (1, 0, 2, 3)).reshape(nps, band, 2 * gathers)


def solution(mesh):
    torus = Mesh(mesh.devices.reshape(mesh.shape["freq"], 4, 8), ("freq", "offset_0", "offset_1"))
    placed = (P(OFFSET, "freq"), P(None, OFFSET), P(), P())
    return jax.shard_map(
        local, mesh=torus, in_specs=placed, out_specs=P(OFFSET, "freq", None), check_vma=False
    )
```

time: 207 us -> 93.6 us (0.45); the launches traced: 203 us -> 93 us
  waiting for transfers between devices: 105 us -> 16 us
  matrix products: 36.9 us -> 6.4 us
  blocking collectives: 0 us -> 15.9 us
  between operations: 13.5 us -> 0.19 us
  starting transfers between devices: 15.3 us -> 26.5 us
  local copies, waits for them, and re-layouts: 18.1 us -> 10 us
  other arithmetic: 14.1 us -> 18 us
    unnamed x3 -> x0, waiting for transfers between devices: 50.5 us -> none
    reduce_scatter x1 -> x0, waiting for transfers between devices: 41.7 us -> none  [own_rows(): total = lax.psum_scatter(total, axis, scatter_dimension=0, tiled=True)]
    dot_general x5, matrix products: 36.9 us -> 6.4 us  [the longest x1 4.96 us: local(): jnp.dot(series, table, preferred_element_type=jnp.float32)]
    all_to_all x0 -> x1, blocking collectives: none -> 15.9 us  [local(): got = lax.all_to_all(panel, OFFSET, split_axis=0, concat_axis=0, tiled=True)]
    all_to_all x0 -> x1, starting transfers between devices: none -> 11.5 us  [local(): lax.all_to_all(first, OFFSET, split_axis=0, concat_axis=0, tiled=True)]
    unnamed x8 -> x6, local copies, waits for them, and re-layouts: 9.12 us -> 0.04 us
    convert_element_type x0 -> x1, other arithmetic: none -> 7.98 us  [local(): sines = jnp.sin(phases).astype(jnp.bfloat16)]
    reduce_scatter x1 -> x0, local copies, waits for them, and re-layouts: 2.72 us -> none  [own_rows(): total = lax.psum_scatter(total, axis, scatter_dimension=0, tiled=True)]
  transfers between devices with their start and end apart: 4 -> 3, of which waited for: 4 -> 3; matrix products, arithmetic and copies ran while one was open for 5% -> 19% of each run, Pallas kernels for 0% -> 0%
where the time goes in v1:
time: 93.6 us; the launch traced here: 93 us
  starting transfers between devices  26.5 us (28%)
  other arithmetic  18 us (19%)
  waiting for transfers between devices  16 us (17%)
  blocking collectives  15.9 us (17%)
  local copies, waits for them, and re-layouts  10 us (11%)
  matrix products  6.4 us (7%)
    all_to_all x1, blocking collectives, local(): got = lax.all_to_all(panel, OFFSET, split_axis=0, concat_axis=0, tiled=True)  15.9 us
    all_to_all x1, waiting for transfers between devices, local(): lax.all_to_all(spectrum, 'freq', split_axis=0, concat_axis=0, tiled=True)  11.5 us
    all_to_all x1, starting transfers between devices, local(): lax.all_to_all(first, OFFSET, split_axis=0, concat_axis=0, tiled=True)  11.5 us
    all_to_all x1, starting transfers between devices, local(): lax.all_to_all(grouped, 'freq', split_axis=0, concat_axis=2, tiled=True)  10.2 us
    convert_element_type x1, other arithmetic, local(): sines = jnp.sin(phases).astype(jnp.bfloat16)  7.98 us
    convert_element_type x1, other arithmetic, whole_table(): return (values * (1.0 / math.sqrt(total_time))).astype(jnp.bfloat16)  6.17 us
    dot_general x1, matrix products, local(): jnp.dot(series, table, preferred_element_type=jnp.float32)  4.96 us
    all_to_all x1, starting transfers between devices, local(): lax.all_to_all(spectrum, 'freq', split_axis=0, concat_axis=0, tiled=True)  4.88 us
  transfers between devices with their start and end apart: 3, of which 3 were waited for; matrix products, arithmetic and copies ran while one was open for 19% of the time, Pallas kernels for 0%

profile of v1, /device:TPU:1, one launch (start us, length us, event | category | flops | bytes accessed | tf_op | source)
XLA Modules:
  0.0 93.0 jit_solution(5154086458202436365)
XLA Ops:
  0.0 0.0 copy-start
  0.0 0.8 copy.25
  0.8 0.1 reshape.312
  0.9 0.0 copy-done
  1.0 4.3 %gather_fusion = bf16[1024,128]{1,0:T(8,128)(2,1)} fusion(bf16[1024,128]{1,0:T(8,128)(2,1)S(1)} %copy-done, s32[1024]{0:T(1024)S(1)} %broadcast_clamp_fusion), kind=kCustom, calls=%fused_computation | custom fusion | bytes 528384 | tf_op jit(solution)/shard_map/gather | solution.py:59
  5.3 10.2 %all-to-all-start = ((bf16[16,64,128]{2,1,0:T(8,128)(2,1)}), bf16[16,64,128]{2,1,0:T(8,128)(2,1)S(1)}, u32[]{:S(2)}, u32[]{:S(2)}) async-start(bf16[16,64,128]{2,1,0:T(8,128)(2,1)} %bitcast.3), calls=%async_computation | async-start | bytes 524288 | tf_op jit(solution)/shard_map/all_to_all | solution.py:62
  15.5 2.1 %fusion.10 = (f32[64,2048]{1,0:T(8,128)S(1)}, f32[64,2048]{1,0:T(8,128)S(1)}) fusion(s32[2048]{0:T(1024)S(1)} %get-tuple-element.16, s32[2048]{0:T(1024)S(1)} %get-tuple-element.15), kind=kLoop, calls=%fused_computation.28 | loop fusion | flops 1966080 | bytes 1064960 | tf_op jit(solution)/shard_map/cos | solution.py:39
  17.5 1.1 %fusion.21 = (f32[32,2048]{1,0:T(8,128)S(1)}, f32[32,2048]{1,0:T(8,128)S(1)}) fusion(s32[2048]{0:T(1024)S(1)} %get-tuple-element.15, s32[32]{0:T(128)S(1)} %and_select_fusion), kind=kLoop, calls=%fused_computation.40 | loop fusion | flops 917504 | bytes 532608 | tf_op jit(solution)/shard_map/cos | solution.py:37
  18.6 6.2 %multiply_convert_fusion = bf16[32,64,2048]{2,1,0:T(8,128)(2,1)} fusion(f32[64,2048]{1,0:T(8,128)S(1)} %get-tuple-element.12, f32[32,2048]{1,0:T(8,128)S(1)} %get-tuple-element.14, f32[64,2048]{1,0:T(8,128)S(1)} %get-tuple-element.11, f32[32,2048]{1,0:T(8,128)S(1)} %get-tuple-element.13), kind=kLoop, calls=%fused_computation.1 | loop fusion | flops 20971520 | bytes 9961472 | tf_op jit(solution)/shard_map/convert_element_type | solution.py:46
  24.8 2.4 %all-to-all-done = bf16[16,64,128]{2,1,0:T(8,128)(2,1)S(1)} async-done(((bf16[16,64,128]{2,1,0:T(8,128)(2,1)}), bf16[16,64,128]{2,1,0:T(8,128)(2,1)S(1)}, u32[]{:S(2)}, u32[]{:S(2)}) %all-to-all-start) | async-done | bytes 262176 | tf_op jit(solution)/shard_map/all_to_all | solution.py:62
  27.2 0.2 copy.26
  27.4 0.0 copy-start.1
  27.4 0.0 copy-start.2
  27.4 5.0 %convolution_convert_fusion = bf16[64,2048]{1,0:T(8,128)(2,1)S(1)} fusion(bf16[2048,2048]{1,0:T(8,128)(2,1)} %bitcast.40, bf16[8,8,16,128]{3,2,1,0:T(8,128)(2,1)S(1)} %bitcast.42), kind=kOutput, calls=%fused_computation.4 | convolution fusion | flops 537001984 | bytes 8912896 | tf_op jit(solution)/shard_map/dot_general | solution.py:64
  32.3 0.3 copy.27
  32.6 0.4 reshape.315
  33.0 0.5 copy.28
  33.5 1.2 %reshape.316 = bf16[16,32,2,128]{3,1,2,0:T(8,128)(2,1)} reshape(bf16[16,32,2,4,32]{4,3,1,2,0:T(4,128)(2,1)S(1)} %copy.28) | data formatting | bytes 524288 | tf_op jit(solution)/shard_map/reshape | solution.py:67
  34.8 4.9 %all-to-all-start.1 = ((bf16[16,32,2,128]{3,1,2,0:T(8,128)(2,1)}), bf16[16,32,2,128]{3,1,2,0:T(8,128)(2,1)S(1)}, u32[]{:S(2)}, u32[]{:S(2)}) async-start(bf16[16,32,2,128]{3,1,2,0:T(8,128)(2,1)} %reshape.316), calls=%async_computation.1 | async-start | bytes 524288 | tf_op jit(solution)/shard_map/all_to_all | solution.py:68
  39.6 0.0 copy-done.1
  39.7 0.0 copy-done.2
  39.7 11.5 %all-to-all-done.1 = bf16[16,32,2,128]{3,1,2,0:T(8,128)(2,1)S(1)} async-done(((bf16[16,32,2,128]{3,1,2,0:T(8,128)(2,1)}), bf16[16,32,2,128]{3,1,2,0:T(8,128)(2,1)S(1)}, u32[]{:S(2)}, u32[]{:S(2)}) %all-to-all-start.1) | async-done | bytes 262176 | tf_op jit(solution)/shard_map/all_to_all | solution.py:68
  51.2 0.8 copy.29
  52.0 11.5 %all-to-all-start.2 = ((bf16[32,32,128]{2,1,0:T(8,128)(2,1)}), bf16[32,32,128]{2,1,0:T(8,128)(2,1)S(1)}, u32[]{:S(2)}, u32[]{:S(2)}) async-start(bf16[32,32,128]{2,1,0:T(8,128)(2,1)} %copy.29), calls=%async_computation.2 | async-start | bytes 524288 | tf_op jit(solution)/shard_map/all_to_all | solution.py:70
  63.5 0.4 sqrt_add_fusion
  64.0 8.0 %fusion.1 = (bf16[2,256,1024]{2,1,0:T(8,128)(2,1)S(1)}, bf16[2,256,1024]{2,1,0:T(8,128)(2,1)S(1)}) fusion(f32[256,1024]{1,0:T(8,128)S(1)} %sqrt_add_fusion, f32[2]{0:T(128)S(1)} %convert_multiply_fusion.1), kind=kLoop, calls=%fused_computation.6 | loop fusion | flops 1572864 | bytes 3145736 | tf_op jit(solution)/shard_map/convert_element_type | solution.py:78
  72.0 2.1 %all-to-all-done.2 = bf16[32,32,128]{2,1,0:T(8,128)(2,1)S(1)} async-done(((bf16[32,32,128]{2,1,0:T(8,128)(2,1)}), bf16[32,32,128]{2,1,0:T(8,128)(2,1)S(1)}, u32[]{:S(2)}, u32[]{:S(2)}) %all-to-all-start.2) | async-done | bytes 262176 | tf_op jit(solution)/shard_map/all_to_all | solution.py:70
  74.0 0.3 fusion.8
  74.3 0.4 fusion.6
  74.8 0.3 fusion.7
  75.0 0.4 fusion.5
  75.5 0.1 copy.30
  75.6 0.1 copy.31
  75.7 0.1 copy.32
  75.8 0.1 copy.33
  75.9 0.2 maximum_multiply_fusion
  76.1 15.9 %all_to_all.30 = f32[32,8,128]{2,1,0:T(8,128)S(1)} all-to-all(f32[32,8,128]{2,1,0:T(8,128)S(1)} %maximum_multiply_fusion), channel_id=1, replica_groups=mesh['freq'=16,'offset_0'=4,'offset_1'=8] {'offset_0','offset_1'}, dimensions={0} | all-to-all | bytes 262144 | tf_op jit(solution)/shard_map/all_to_all | solution.py:91
  92.0 0.2 reshape.319
  92.2 0.8 copy.34
  (9 shorter events, 0.1 us)
Async XLA Ops:
  0.0 1.0 %copy-start = (bf16[1024,128]{1,0:T(8,128)(2,1)S(1)}, bf16[1024,128]{1,0:T(8,128)(2,1)}, u32[]{:S(2)}) copy-start(bf16[1024,128]{1,0:T(8,128)(2,1)} %param.4) | copy-start | bytes 786436
  5.3 21.9 %all-to-all-start = ((bf16[16,64,128]{2,1,0:T(8,128)(2,1)}), bf16[16,64,128]{2,1,0:T(8,128)(2,1)S(1)}, u32[]{:S(2)}, u32[]{:S(2)}) async-start(bf16[16,64,128]{2,1,0:T(8,128)(2,1)} %bitcast.3), calls=%async_computation | async-start | bytes 524288 | tf_op jit(solution)/shard_map/all_to_all | solution.py:62
  27.4 12.3 %copy-start.1 = (s32[1024]{0:T(1024)S(1)}, s32[1024]{0:T(1024)}, u32[]{:S(2)}) copy-start(s32[1024]{0:T(1024)} %param.6) | copy-start | bytes 12292
  27.4 12.3 %copy-start.2 = (s32[256]{0:T(256)S(1)}, s32[256]{0:T(256)}, u32[]{:S(2)}) copy-start(s32[256]{0:T(256)} %param.7) | copy-start | bytes 3076
  34.8 16.5 %all-to-all-start.1 = ((bf16[16,32,2,128]{3,1,2,0:T(8,128)(2,1)}), bf16[16,32,2,128]{3,1,2,0:T(8,128)(2,1)S(1)}, u32[]{:S(2)}, u32[]{:S(2)}) async-start(bf16[16,32,2,128]{3,1,2,0:T(8,128)(2,1)} %reshape.316), calls=%async_computation.1 | async-start | bytes 524288 | tf_op jit(solution)/shard_map/all_to_all | solution.py:68
  52.0 22.0 %all-to-all-start.2 = ((bf16[32,32,128]{2,1,0:T(8,128)(2,1)}), bf16[32,32,128]{2,1,0:T(8,128)(2,1)S(1)}, u32[]{:S(2)}, u32[]{:S(2)}) async-start(bf16[32,32,128]{2,1,0:T(8,128)(2,1)} %copy.29), calls=%async_computation.2 | async-start | bytes 524288 | tf_op jit(solution)/shard_map/all_to_all | solution.py:70

commit v2 on v1

v2 whole, which is shorter than its diff:
```python
import functools
import math

import jax
import jax.numpy as jnp
import numpy as np
from jax import lax
from jax.experimental import pallas as pl
from jax.experimental.pallas import tpu as pltpu
from jax.sharding import PartitionSpec as P

NT = 2048
NF = 1024
NP = 256
G = 32
HB = 32
NH = 1024
NK = 16
NO = 32
NX = 4
NZ = 8
APEX_TIME = 100.0
CURVATURE = 0.0003
MESH = pl.DeviceIdType.MESH
F32 = jnp.float32
BF16 = jnp.bfloat16


def dft_tables():
    n = np.arange(256)[None, :]
    a = np.arange(128)[:, None]
    t0 = 2 * np.pi * ((a * n) % 256) / 256
    t1 = 2 * np.pi * (((255 - a) * n) % 256) / 256
    rows = [
        np.concatenate([np.cos(t0), np.sin(t0)], 1),
        np.concatenate([-np.sin(t0), np.cos(t0)], 1),
        np.concatenate([np.cos(t1), np.sin(t1)], 1),
        np.concatenate([np.sin(t1), -np.cos(t1)], 1),
    ]
    table = np.concatenate(rows, 0)
    m = 2 * np.arange(4)[:, None] + 1
    turn = np.pi * (m * n) / 2048
    twiddle = np.concatenate([np.cos(turn), np.sin(turn)], 0) / math.sqrt(NT)
    return table.astype(np.float32), twiddle.astype(np.float32)


def half_turn_fit(odd, terms):
    nodes = 0.25 * (np.cos(np.pi * (np.arange(400) + 0.5) / 400) + 1) / 2
    r = np.sqrt(nodes)
    want = np.sin(np.pi * r) / r if odd else np.cos(np.pi * r)
    fit = np.polynomial.chebyshev.Chebyshev.fit(nodes, want, terms - 1, domain=[0, 0.25])
    return [float(v) for v in fit.convert(kind=np.polynomial.Polynomial).coef]


SIN_FIT = half_turn_fit(True, 6)
COS_FIT = half_turn_fit(False, 6)


def horner(x, coef):
    total = coef[-1] * x + coef[-2]
    for value in coef[-3::-1]:
        total = total * x + value
    return total


def far_first(i, n):
    half = n // 2
    return half + ((i + 1) // 2) * (1 - 2 * (i % 2))


def kernel(raw, slot, offs, slow, twid, table_hbm, out,
           table, send_a, recv_a, spec, send_b, recv_b, wide, send_c, recv_c, weights, curve,
           send_d, recv_d,
           ssem_a, rsem_a, ssem_b, rsem_b, ssem_c, rsem_c, ssem_d, rsem_d, table_sem):
    me_k = lax.axis_index("freq")
    me_o = lax.axis_index("offset")
    me_x, me_z = me_o // NZ, me_o % NZ

    def peer_k(i):
        return (me_k + far_first(i, NK)) % NK

    def peer_o(i):
        dz = far_first(i // NX, NZ)
        dx = far_first(i % NX, NX)
        return ((me_x + dx) % NX) * NZ + (me_z + dz) % NZ

    barrier = pltpu.get_barrier_semaphore()

    def greet_k(i, c):
        pl.semaphore_signal(barrier, inc=1, device_id=(peer_k(i), me_o), device_id_type=MESH)
        return c

    def greet_o(i, c):
        pl.semaphore_signal(barrier, inc=1, device_id=(me_k, peer_o(i)), device_id_type=MESH)
        return c

    lax.fori_loop(0, NO - 1, greet_o, 0)
    lax.fori_loop(0, NK - 1, greet_k, 0)
    table_copy = pltpu.make_async_copy(table_hbm, table, table_sem)
    table_copy.start()

    lane_ids = lax.broadcasted_iota(jnp.int32, (G, HB * G), 1)
    data = raw[...]
    for kk in range(NK):
        picks = [
            jnp.where(slot[:, 2 * kk + h:2 * kk + h + 1] == lane_ids, 1.0, 0.0) for h in range(2)
        ]
        chosen = jnp.concatenate(picks, axis=0).astype(BF16)
        send_a[kk] = jnp.dot(chosen, data, preferred_element_type=F32).astype(BF16)

    pl.semaphore_wait(barrier, NO - 1 + NK - 1)

    def copy_k(src, dst, ssem, rsem, there, here):
        return pltpu.make_async_remote_copy(
            src_ref=src.at[there], dst_ref=dst.at[here], send_sem=ssem.at[there],
            recv_sem=rsem.at[here], device_id=(there, me_o), device_id_type=MESH)

    def copy_o(src, dst, ssem, rsem, there, here):
        return pltpu.make_async_remote_copy(
            src_ref=src.at[there], dst_ref=dst.at[here], send_sem=ssem.at[there],
            recv_sem=rsem.at[here], device_id=(me_k, there), device_id_type=MESH)

    def start_all(make, count, peer, me, *refs):
        def step(i, c):
            make(*refs, peer(i), me).start()
            return c
        lax.fori_loop(0, count, step, 0)

    def await_recv(make, count, peer, *refs):
        def step(i, c):
            make(*refs, peer(i), peer(i)).wait_recv()
            return c
        lax.fori_loop(0, count, step, 0)

    def await_send(make, count, peer, me, *refs):
        def step(i, c):
            make(*refs, peer(i), me).wait_send()
            return c
        lax.fori_loop(0, count, step, 0)

    a_refs = (send_a, recv_a, ssem_a, rsem_a)
    b_refs = (send_b, recv_b, ssem_b, rsem_b)
    c_refs = (send_c, recv_c, ssem_c, rsem_c)
    d_refs = (send_d, recv_d, ssem_d, rsem_d)

    start_all(copy_k, NK - 1, peer_k, me_k, *a_refs)
    recv_a[me_k] = send_a[me_k]

    for half in range(2):
        row = slow[:, 128 * half:128 * half + 128].astype(F32) * CURVATURE
        curve[128 * half:128 * half + 128, :] = jnp.transpose(jnp.broadcast_to(row, (128, 128)))
    first = 64 * me_k + 8 * me_z + me_x
    second = 64 * me_k + 8 * me_z + 7 - me_x
    rates = [(2 * f + 1).astype(F32) * (1.0 / (2 * NT)) for f in (first, second)]

    def weigh(block, c):
        rows = pl.ds(pl.multiple_of(block * 16, 16), 16)
        low = pl.ds(pl.multiple_of(block * 16 + NP, 16), 16)
        steep = curve[rows, :]
        for part in range(NH // 256):
            lanes = slice(256 * part, 256 * part + 256)
            spread = jnp.concatenate([steep, steep], axis=1) * offs[:, lanes].astype(F32)
            delay = jnp.sqrt(APEX_TIME * APEX_TIME + spread * spread) - APEX_TIME
            for f in range(2):
                turns = delay * rates[f]
                r = turns - jnp.round(turns)
                r2 = r * r
                s = horner(r2, SIN_FIT) * r
                q = horner(r2, COS_FIT)
                weights[f, rows, lanes] = (1.0 - 2.0 * (s * s)).astype(BF16)
                weights[f, low, lanes] = (2.0 * (s * q)).astype(BF16)
        return c

    lax.fori_loop(0, NP // 16, weigh, 0)

    await_recv(copy_k, NK - 1, peer_k, *a_refs)

    x = [jnp.concatenate([recv_a[2 * d], recv_a[2 * d + 1]], axis=1).astype(F32) for d in range(8)]
    less = [x[d] - x[8 - d] for d in range(1, 4)]
    more = [x[d] + x[8 - d] for d in range(1, 4)]
    for b in range(4):
        m = 2 * b + 1
        yr = x[0]
        yi = x[4] * (-math.sin(math.pi * m / 2))
        for d in range(1, 4):
            yr = yr + less[d - 1] * math.cos(math.pi * d * m / 8)
            yi = yi - more[d - 1] * math.sin(math.pi * d * m / 8)
        tc = twid[b:b + 1, :]
        ts = twid[4 + b:5 + b, :]
        spec[64 * b:64 * b + 64, 0:256] = (yr * tc + yi * ts).astype(BF16)
        spec[64 * b:64 * b + 64, 256:512] = (yi * tc - yr * ts).astype(BF16)
    table_copy.wait()
    lane = lax.broadcasted_iota(jnp.int32, (128, 128), 1) // 32
    spec_all = spec[...]
    parts = [
        lax.dot_general(table[128 * c:128 * c + 128, :], spec_all, (((1,), (1,)), ((), ())),
                        preferred_element_type=F32)
        for c in range(4)
    ]
    for tile in range(2):
        pieces = [p[:, 128 * tile:128 * tile + 128] for p in parts]
        for h in range(2):
            both = []
            for b in range(2):
                i = 2 * b + h
                total = pieces[0] if i == 0 else pltpu.roll(pieces[0], (0 - i) * 32 % 128, 1)
                for c in range(1, 4):
                    moved = pieces[c] if c == i else pltpu.roll(pieces[c], (c - i) * 32 % 128, 1)
                    total = jnp.where(lane == c, moved, total)
                both.append(total.reshape(NK, 8, 128))
            rows = slice(32 * h + 16 * tile, 32 * h + 16 * tile + 16)
            send_b[:, rows, :] = jnp.concatenate(both, axis=1).astype(BF16)

    start_all(copy_k, NK - 1, peer_k, me_k, *b_refs)
    recv_b[me_k] = send_b[me_k]
    await_recv(copy_k, NK - 1, peer_k, *b_refs)

    wide[...] = recv_b[...].astype(F32).reshape(NK * 64, 128)
    for q in range(NO):
        send_c[q] = wide[pl.ds(q, 32, stride=32), :].astype(BF16)
    start_all(copy_o, NO - 1, peer_o, me_o, *c_refs)
    recv_c[me_o] = send_c[me_o]
    await_recv(copy_o, NO - 1, peer_o, *c_refs)

    spectra = recv_c[...].reshape(NH, 128)
    lane = lax.broadcasted_iota(jnp.int32, (64, 128), 1)
    for block in range(NP // 64):
        rows = slice(64 * block, 64 * block + 64)
        low = slice(NP + 64 * block, NP + 64 * block + 64)
        cosine = [jnp.dot(weights[f, rows, :], spectra, preferred_element_type=F32) for f in range(2)]
        sines = [jnp.dot(weights[f, low, :], spectra, preferred_element_type=F32) for f in range(2)]
        ca = jnp.where(lane < 64, cosine[0], cosine[1])
        sa = jnp.where(lane < 64, sines[0], sines[1])
        swapped = jnp.where(lane % 64 < 32, -pltpu.roll(sa, 96, 1), pltpu.roll(sa, 32, 1))
        panel = (ca + swapped) * (1.0 / math.sqrt(NH))
        send_d[8 * block:8 * block + 8] = panel.reshape(8, 8, 128)

    start_all(copy_o, NO - 1, peer_o, me_o, *d_refs)
    recv_d[me_o] = send_d[me_o]
    await_recv(copy_o, NO - 1, peer_o, *d_refs)
    for o in range(NO):
        one = recv_d[o]
        f0 = 8 * (o % NZ) + o // NZ
        f1 = 8 * (o % NZ) + 7 - o // NZ
        out[pl.ds(f0, 8, stride=64), :] = one[:, 0:64]
        out[pl.ds(f1, 8, stride=64), :] = one[:, 64:128]

    await_send(copy_k, NK - 1, peer_k, me_k, *a_refs)
    await_send(copy_k, NK - 1, peer_k, me_k, *b_refs)
    await_send(copy_o, NO - 1, peer_o, me_o, *c_refs)
    await_send(copy_o, NO - 1, peer_o, me_o, *d_refs)


def local(raw_traces, trace_slot, offset_index, slowness_index):
    table, twiddle = dft_tables()
    vmem = pl.BlockSpec(memory_space=pltpu.VMEM)
    dma = pltpu.SemaphoreType.DMA
    got = pl.pallas_call(
        kernel,
        out_shape=jax.ShapeDtypeStruct((8 * 64, 64), F32),
        in_specs=[vmem] * 5 + [pl.BlockSpec(memory_space=pl.ANY)],
        out_specs=vmem,
        scratch_shapes=[
            pltpu.VMEM((512, 512), BF16),
            pltpu.VMEM((NK, 64, 128), BF16), pltpu.VMEM((NK, 64, 128), BF16),
            pltpu.VMEM((256, 512), BF16),
            pltpu.VMEM((NK, 64, 128), BF16), pltpu.VMEM((NK, 64, 128), BF16),
            pltpu.VMEM((NK * 64, 128), F32),
            pltpu.VMEM((NO, 32, 128), BF16), pltpu.VMEM((NO, 32, 128), BF16),
            pltpu.VMEM((2, 2 * NP, NH), BF16),
            pltpu.VMEM((NP, 128), F32),
            pltpu.VMEM((NO, 8, 128), F32), pltpu.VMEM((NO, 8, 128), F32),
            dma((NK,)), dma((NK,)), dma((NK,)), dma((NK,)),
            dma((NO,)), dma((NO,)), dma((NO,)), dma((NO,)), dma(()),
        ],
        compiler_params=pltpu.CompilerParams(
            collective_id=0, has_side_effects=True, vmem_limit_bytes=32 * 1024 * 1024),
        name="radon",
    )(raw_traces, trace_slot, offset_index.reshape(1, NH), slowness_index.reshape(1, NP),
      jnp.asarray(twiddle), jnp.asarray(table, dtype=BF16))
    return got.reshape(8, 64, 64)


def solution(mesh):
    placed = (P("offset", "freq"), P(None, "offset"), P(), P())
    return jax.shard_map(
        local, mesh=mesh, in_specs=placed, out_specs=P("offset", "freq", None), check_vma=False
    )
```

time: 93.6 us -> 59.3 us (0.63)
  Pallas kernels: 0 us -> 53.3 us
  starting transfers between devices: 26.5 us -> 0 us
  other arithmetic: 18 us -> 0 us
  waiting for transfers between devices: 16 us -> 0 us
  blocking collectives: 15.9 us -> 0 us
  matrix products: 6.4 us -> 0 us
  local copies, waits for them, and re-layouts: 10 us -> 5.47 us
    pallas_call x0 -> x1, Pallas kernels: none -> 53.3 us  [local(): pl.pallas_call(kernel, out_shape=jax.ShapeDtypeStruct((8 * 64, 64), F32),...]
    all_to_all x3 -> x0, starting transfers between devices: 26.5 us -> none  [the longest x1 11.5 us: local(): lax.all_to_all(first, OFFSET, split_axis=0, concat_axis=0, tiled=True)]
    all_to_all x3 -> x0, waiting for transfers between devices: 16 us -> none  [the longest x1 11.5 us: local(): lax.all_to_all(spectrum, 'freq', split_axis=0, concat_axis=0, tiled=True)]
    all_to_all x1 -> x0, blocking collectives: 15.9 us -> none  [local(): got = lax.all_to_all(panel, OFFSET, split_axis=0, concat_axis=0, tiled=True)]
    convert_element_type x3 -> x0, other arithmetic: 14.2 us -> none  [the longest x1 7.98 us: local(): sines = jnp.sin(phases).astype(jnp.bfloat16)]
    dot_general x5 -> x0, matrix products: 6.4 us -> none  [the longest x1 4.96 us: local(): jnp.dot(series, table, preferred_element_type=jnp.float32)]
    unnamed x6 -> x13, local copies, waits for them, and re-layouts: 0.04 us -> 5.47 us
    gather x1 -> x0, local copies, waits for them, and re-layouts: 4.3 us -> none  [local(): picked = raw_traces[trace_slot.T.reshape(-1)]]
  transfers between devices with their start and end apart: 3 -> 0, of which waited for: 3 -> 0; matrix products, arithmetic and copies ran while one was open for 19% -> 0% of each run, Pallas kernels for 0% -> 0%
where the time goes in v2:
time: 59.3 us; the launch traced here: 58.8 us
  Pallas kernels  53.3 us (90%)
  local copies, waits for them, and re-layouts  5.47 us (9%)
    pallas_call x1, Pallas kernels, local(): pl.pallas_call(kernel, out_shape=jax.ShapeDtypeStruct((8 * 64, 64), F32),...  53.3 us
    unnamed x13, local copies, waits for them, and re-layouts  5.47 us

profile of v2, /device:TPU:1, one launch (start us, length us, event | category | flops | bytes accessed | tf_op | source)
XLA Modules:
  0.0 58.8 jit_solution(1917571287960251422)
XLA Ops:
  0.0 0.0 copy-start.5
  0.0 0.7 %copy-done.5 = s32[256]{0:T(256)S(1)} copy-done((s32[256]{0:T(256)S(1)}, s32[256]{0:T(256)}, u32[]{:S(2)}) %copy-start.5) | copy-done | bytes 1048
  0.7 0.0 copy-start
  0.7 1.0 %copy-done = bf16[512,512]{1,0:T(8,128)(2,1)S(1)} copy-done((bf16[512,512]{1,0:T(8,128)(2,1)S(1)}, bf16[512,512]{1,0:T(8,128)(2,1)}, u32[]{:S(2)}) %copy-start) | copy-done | bytes 524312
  1.7 0.0 copy-start.1
  1.7 0.9 %copy-done.1 = bf16[1024,128]{1,0:T(8,128)(2,1)S(1)} copy-done((bf16[1024,128]{1,0:T(8,128)(2,1)S(1)}, bf16[1024,128]{1,0:T(8,128)(2,1)}, u32[]{:S(2)}) %copy-start.1) | copy-done | bytes 262168
  2.7 0.0 copy-start.2
  2.7 0.7 %copy-done.2 = s32[32,32]{1,0:T(8,128)S(1)} copy-done((s32[32,32]{1,0:T(8,128)S(1)}, s32[32,32]{1,0:T(8,128)}, u32[]{:S(2)}) %copy-start.2) | copy-done | bytes 4120
  3.4 0.0 copy-start.3
  3.4 0.7 %copy-done.3 = f32[8,256]{1,0:T(8,128)S(1)} copy-done((f32[8,256]{1,0:T(8,128)S(1)}, f32[8,256]{1,0:T(8,128)}, u32[]{:S(2)}) %copy-start.3) | copy-done | bytes 8216
  4.1 0.0 copy-start.4
  4.1 0.7 %copy-done.4 = s32[1024]{0:T(1024)S(1)} copy-done((s32[1024]{0:T(1024)S(1)}, s32[1024]{0:T(1024)}, u32[]{:S(2)}) %copy-start.4) | copy-done | bytes 4120
  4.8 53.3 %radon.1 = f32[512,64]{1,0:T(8,128)S(1)} custom-call(bf16[1024,128]{1,0:T(8,128)(2,1)S(1)} %copy-done.1, s32[32,32]{1,0:T(8,128)S(1)} %copy-done.2, s32[1,1024]{1,0:T(1,128)S(1)} %bitcast.4, s32[1,256]{1,0:T(1,128)S(1)} %bitcast.5, f32[8,256]{1,0:T(8,128)S(1)} %copy-done.3, bf16[512,512]{1,0:T(8,128)(2,1)S(1)} %copy-done), custom_call_target="tpu_custom_call" | custom-call | tf_op jit(solution)/shard_map/radon/pallas_call | solution.py:258
  58.1 0.7 %copy.8 = f32[8,64,64]{2,1,0:T(8,128)} copy(f32[8,64,64]{2,1,0:T(8,128)S(1)} %bitcast.3) | data formatting | bytes 262144
Async XLA Ops:
  0.0 0.7 %copy-start.5 = (s32[256]{0:T(256)S(1)}, s32[256]{0:T(256)}, u32[]{:S(2)}) copy-start(s32[256]{0:T(256)} %param.9) | copy-start | bytes 3076
  0.7 1.0 %copy-start = (bf16[512,512]{1,0:T(8,128)(2,1)S(1)}, bf16[512,512]{1,0:T(8,128)(2,1)}, u32[]{:S(2)}) copy-start(bf16[512,512]{1,0:T(8,128)(2,1)} %constant.5.clone.table_hbm) | copy-start | bytes 1572868
  1.7 0.9 %copy-start.1 = (bf16[1024,128]{1,0:T(8,128)(2,1)S(1)}, bf16[1024,128]{1,0:T(8,128)(2,1)}, u32[]{:S(2)}) copy-start(bf16[1024,128]{1,0:T(8,128)(2,1)} %raw.1) | copy-start | bytes 786436
  2.7 0.7 %copy-start.2 = (s32[32,32]{1,0:T(8,128)S(1)}, s32[32,32]{1,0:T(8,128)}, u32[]{:S(2)}) copy-start(s32[32,32]{1,0:T(8,128)} %slot.1) | copy-start | bytes 12292
  3.4 0.7 %copy-start.3 = (f32[8,256]{1,0:T(8,128)S(1)}, f32[8,256]{1,0:T(8,128)}, u32[]{:S(2)}) copy-start(f32[8,256]{1,0:T(8,128)} %constant.4.clone.twid) | copy-start | bytes 24580
  4.1 0.7 %copy-start.4 = (s32[1024]{0:T(1024)S(1)}, s32[1024]{0:T(1024)}, u32[]{:S(2)}) copy-start(s32[1024]{0:T(1024)} %param.8) | copy-start | bytes 12292

commit v3 on v2

v3 whole, which is shorter than its diff:
```python
import functools
import math

import jax
import jax.numpy as jnp
import numpy as np
from jax import lax
from jax.experimental import pallas as pl
from jax.experimental.pallas import tpu as pltpu
from jax.sharding import PartitionSpec as P

NT = 2048
NF = 1024
NP = 256
G = 32
HB = 32
NH = 1024
NK = 16
NO = 32
NX = 4
NZ = 8
APEX_TIME = 100.0
CURVATURE = 0.0003
MESH = pl.DeviceIdType.MESH
F32 = jnp.float32
BF16 = jnp.bfloat16


def dft_tables():
    n = np.arange(256)[None, :]
    row = np.arange(128)
    a = (row % NK * NZ + row // NK)[:, None]
    t0 = 2 * np.pi * ((a * n) % 256) / 256
    t1 = 2 * np.pi * (((255 - a) * n) % 256) / 256
    rows = [
        np.concatenate([np.cos(t0), np.sin(t0)], 1),
        np.concatenate([-np.sin(t0), np.cos(t0)], 1),
        np.concatenate([np.cos(t1), np.sin(t1)], 1),
        np.concatenate([np.sin(t1), -np.cos(t1)], 1),
    ]
    table = np.concatenate(rows, 0)
    m = 2 * np.arange(4)[:, None] + 1
    turn = np.pi * (m * n) / 2048
    twiddle = np.concatenate([np.cos(turn), np.sin(turn)], 0) / math.sqrt(NT)
    return table.astype(np.float32), twiddle.astype(np.float32)


def half_turn_fit(odd, terms):
    nodes = 0.25 * (np.cos(np.pi * (np.arange(400) + 0.5) / 400) + 1) / 2
    r = np.sqrt(nodes)
    want = np.sin(np.pi * r) / r if odd else np.cos(np.pi * r)
    fit = np.polynomial.chebyshev.Chebyshev.fit(nodes, want, terms - 1, domain=[0, 0.25])
    return [float(v) for v in fit.convert(kind=np.polynomial.Polynomial).coef]


SIN_FIT = half_turn_fit(True, 6)
COS_FIT = half_turn_fit(False, 6)


def horner(x, coef):
    total = coef[-1] * x + coef[-2]
    for value in coef[-3::-1]:
        total = total * x + value
    return total


def far_first(i, n):
    half = n // 2
    return half + ((i + 1) // 2) * (1 - 2 * (i % 2))


def kernel(raw_hbm, slot_hbm, offs_hbm, slow_hbm, twid_hbm, table_hbm, out,
           raw, slot, offs, slow, twid, table, send_a, recv_a, spec, send_c, recv_c, wide,
           send_b, recv_b, columns, spectra, weights, curve, send_d, recv_d,
           ssem_a, rsem_a, ssem_b, rsem_b, ssem_c, rsem_c, ssem_d, rsem_d, load_sems):
    me_k = lax.axis_index("freq")
    me_o = lax.axis_index("offset")
    me_x, me_z = me_o // NZ, me_o % NZ

    def peer_k(i):
        return (me_k + far_first(i, NK)) % NK

    def peer_o(i):
        dz = far_first(i // NX, NZ)
        dx = far_first(i % NX, NX)
        return ((me_x + dx) % NX) * NZ + (me_z + dz) % NZ

    loads = [
        pltpu.make_async_copy(src, dst, load_sems.at[i])
        for i, (src, dst) in enumerate([
            (slot_hbm, slot), (raw_hbm, raw), (offs_hbm, offs), (slow_hbm, slow),
            (twid_hbm, twid), (table_hbm, table)])
    ]
    for load in loads:
        load.start()
    barrier = pltpu.get_barrier_semaphore()

    def greet_k(i, c):
        pl.semaphore_signal(barrier, inc=1, device_id=(peer_k(i), me_o), device_id_type=MESH)
        return c

    def greet_o(i, c):
        pl.semaphore_signal(barrier, inc=1, device_id=(me_k, peer_o(i)), device_id_type=MESH)
        return c

    lax.fori_loop(0, NO - 1, greet_o, 0)
    lax.fori_loop(0, NK - 1, greet_k, 0)

    def copy_k(src, dst, ssem, rsem, there, here):
        return pltpu.make_async_remote_copy(
            src_ref=src.at[there], dst_ref=dst.at[here], send_sem=ssem.at[there],
            recv_sem=rsem.at[here], device_id=(there, me_o), device_id_type=MESH)

    def copy_o(src, dst, ssem, rsem, there, here):
        return pltpu.make_async_remote_copy(
            src_ref=src.at[there], dst_ref=dst.at[here], send_sem=ssem.at[there],
            recv_sem=rsem.at[here], device_id=(me_k, there), device_id_type=MESH)

    class Exchange:
        def __init__(self, over_freq, *refs):
            self.make, self.count, self.peer, self.me = (
                (copy_k, NK - 1, peer_k, me_k) if over_freq else (copy_o, NO - 1, peer_o, me_o))
            self.refs = refs

        def each(self, act):
            def step(i, c):
                act(self.peer(i))
                return c
            lax.fori_loop(0, self.count, step, 0)

        def start(self):
            self.each(lambda there: self.make(*self.refs, there, self.me).start())
            self.refs[1][self.me] = self.refs[0][self.me]

        def arrive(self):
            self.each(lambda there: self.make(*self.refs, there, there).wait_recv())

        def leave(self):
            self.each(lambda there: self.make(*self.refs, there, self.me).wait_send())

    def halves(over_freq, *refs):
        return [Exchange(over_freq, *(ref.at[h] for ref in refs)) for h in range(2)]

    ex_a = halves(True, send_a, recv_a, ssem_a, rsem_a)
    ex_b = halves(True, send_b, recv_b, ssem_b, rsem_b)
    ex_c = halves(False, send_c, recv_c, ssem_c, rsem_c)
    ex_d = Exchange(False, send_d, recv_d, ssem_d, rsem_d)

    loads[0].wait()
    loads[1].wait()
    row_ids = lax.broadcasted_iota(jnp.int32, (G, HB * G), 1)

    def pick(h):
        for part in range(2):
            chosen = jnp.concatenate([
                jnp.where(slot[:, 2 * kk + h:2 * kk + h + 1] == row_ids, 1.0, 0.0).astype(BF16)
                for kk in range(8 * part, 8 * part + 8)
            ], axis=0)
            rows = jnp.dot(chosen, raw[...], preferred_element_type=F32).astype(BF16)
            send_a[h, 8 * part:8 * part + 8] = rows.reshape(8, G, 128)

    pick(0)
    pl.semaphore_wait(barrier, NO - 1 + NK - 1)
    ex_a[0].start()
    pick(1)
    ex_a[1].start()

    loads[2].wait()
    loads[3].wait()
    for half in range(2):
        row = slow[:, 128 * half:128 * half + 128].astype(F32) * CURVATURE
        curve[128 * half:128 * half + 128, :] = jnp.transpose(jnp.broadcast_to(row, (128, 128)))
    first = 64 * me_k + 8 * me_z + me_x
    second = 64 * me_k + 8 * me_z + 7 - me_x
    rates = [(2 * f + 1).astype(F32) * (1.0 / (2 * NT)) for f in (first, second)]

    def weigh(block, c):
        rows = pl.ds(pl.multiple_of(block * 16, 16), 16)
        low = pl.ds(pl.multiple_of(block * 16 + NP, 16), 16)
        steep = curve[rows, :]
        for part in range(NH // 256):
            lanes = slice(256 * part, 256 * part + 256)
            spread = jnp.concatenate([steep, steep], axis=1) * offs[:, lanes].astype(F32)
            delay = jnp.sqrt(APEX_TIME * APEX_TIME + spread * spread) - APEX_TIME
            for f in range(2):
                turns = delay * rates[f]
                r = turns - jnp.round(turns)
                r2 = r * r
                s = horner(r2, SIN_FIT) * r
                q = horner(r2, COS_FIT)
                weights[f, rows, lanes] = (1.0 - 2.0 * (s * s)).astype(BF16)
                weights[f, low, lanes] = (2.0 * (s * q)).astype(BF16)
        return c

    lax.fori_loop(0, NP // 16, weigh, 0)
    loads[4].wait()
    loads[5].wait()

    lane = lax.broadcasted_iota(jnp.int32, (128, 128), 1) // 32

    def transform(h):
        x = [
            jnp.concatenate([recv_a[h, 2 * d], recv_a[h, 2 * d + 1]], axis=1).astype(F32)
            for d in range(8)
        ]
        less = [x[d] - x[8 - d] for d in range(1, 4)]
        more = [x[d] + x[8 - d] for d in range(1, 4)]
        for b in range(4):
            m = 2 * b + 1
            yr = x[0]
            yi = x[4] * (-math.sin(math.pi * m / 2))
            for d in range(1, 4):
                yr = yr + less[d - 1] * math.cos(math.pi * d * m / 8)
                yi = yi - more[d - 1] * math.sin(math.pi * d * m / 8)
            tc = twid[b:b + 1, :]
            ts = twid[4 + b:5 + b, :]
            for side, value in enumerate([yr * tc + yi * ts, yi * tc - yr * ts]):
                high = value.astype(BF16)
                rest = (value - high.astype(F32)).astype(BF16)
                lanes = slice(256 * side, 256 * side + 256)
                spec[G * b:G * b + G, lanes] = high
                spec[128 + G * b:128 + G * b + G, lanes] = rest
        parts = []
        for c in range(4):
            both = lax.dot_general(table[128 * c:128 * c + 128, :], spec[...],
                                   (((1,), (1,)), ((), ())), preferred_element_type=F32)
            parts.append(both[:, 0:128] + both[:, 128:256])
        for b in range(4):
            total = None
            for c in range(4):
                moved = parts[c] if c == b else pltpu.roll(parts[c], (c - b) * 32 % 128, 1)
                total = moved if c == 0 else jnp.where(lane == c, moved, total)
            send_c[h, 8 * b:8 * b + 8] = total.reshape(NZ, NK, 128).astype(BF16)

    def regroup(h):
        wide[...] = recv_c[h].astype(F32).reshape(NO * NK, 128)
        for kk in range(NK):
            send_b[h, kk] = wide[pl.ds(kk, NO, stride=NK), :].astype(BF16)

    for h in range(2):
        ex_a[h].arrive()
        transform(h)
        ex_c[h].start()
    for h in range(2):
        ex_c[h].arrive()
        regroup(h)
        ex_b[h].start()
    for h in range(2):
        ex_b[h].arrive()
        for kk in range(NK):
            base = 2 * NO * kk + NO * h
            columns[base:base + NO, :] = recv_b[h, kk].astype(F32)
    for o in range(NO):
        spectra[HB * o:HB * o + HB, :] = columns[pl.ds(o, HB, stride=NO), :].astype(BF16)

    lane2 = lax.broadcasted_iota(jnp.int32, (64, 128), 1)
    for block in range(NP // 64):
        rows = slice(64 * block, 64 * block + 64)
        low = slice(NP + 64 * block, NP + 64 * block + 64)
        data = spectra[...]
        cosine = [jnp.dot(weights[f, rows, :], data, preferred_element_type=F32) for f in range(2)]
        sines = [jnp.dot(weights[f, low, :], data, preferred_element_type=F32) for f in range(2)]
        ca = jnp.where(lane2 < 64, cosine[0], cosine[1])
        sa = jnp.where(lane2 < 64, sines[0], sines[1])
        swapped = jnp.where(lane2 % 64 < 32, -pltpu.roll(sa, 96, 1), pltpu.roll(sa, 32, 1))
        panel = (ca + swapped) * (1.0 / math.sqrt(NH))
        send_d[8 * block:8 * block + 8] = panel.reshape(8, 8, 128).astype(send_d.dtype)

    ex_d.start()
    ex_d.arrive()
    for o in range(NO):
        one = recv_d[o].astype(F32)
        f0 = 8 * (o % NZ) + o // NZ
        f1 = 8 * (o % NZ) + 7 - o // NZ
        out[pl.ds(f0, 8, stride=64), :] = one[:, 0:64]
        out[pl.ds(f1, 8, stride=64), :] = one[:, 64:128]

    for ex in ex_a + ex_b + ex_c + [ex_d]:
        ex.leave()


def local(raw_traces, trace_slot, offset_index, slowness_index):
    table, twiddle = dft_tables()
    dma = pltpu.SemaphoreType.DMA
    got = pl.pallas_call(
        kernel,
        out_shape=jax.ShapeDtypeStruct((8 * 64, 64), F32),
        in_specs=[pl.BlockSpec(memory_space=pltpu.HBM)] * 6,
        out_specs=pl.BlockSpec(memory_space=pltpu.VMEM),
        scratch_shapes=[
            pltpu.VMEM((HB * G, 128), BF16), pltpu.VMEM((G, HB), jnp.int32),
            pltpu.VMEM((1, NH), jnp.int32), pltpu.VMEM((1, NP), jnp.int32),
            pltpu.VMEM((8, 256), F32), pltpu.VMEM((512, 512), BF16),
            pltpu.VMEM((2, NK, G, 128), BF16), pltpu.VMEM((2, NK, G, 128), BF16),
            pltpu.VMEM((256, 512), BF16),
            pltpu.VMEM((2, NO, NK, 128), BF16), pltpu.VMEM((2, NO, NK, 128), BF16),
            pltpu.VMEM((NO * NK, 128), F32),
            pltpu.VMEM((2, NK, NO, 128), BF16), pltpu.VMEM((2, NK, NO, 128), BF16),
            pltpu.VMEM((NK * 2 * NO, 128), F32), pltpu.VMEM((NH, 128), BF16),
            pltpu.VMEM((2, 2 * NP, NH), BF16),
            pltpu.VMEM((NP, 128), F32),
            pltpu.VMEM((NO, 8, 128), BF16), pltpu.VMEM((NO, 8, 128), BF16),
            dma((2, NK)), dma((2, NK)), dma((2, NK)), dma((2, NK)),
            dma((2, NO)), dma((2, NO)), dma((NO,)), dma((NO,)), dma((6,)),
        ],
        compiler_params=pltpu.CompilerParams(collective_id=0, has_side_effects=True),
        name="radon",
    )(raw_traces, trace_slot, offset_index.reshape(1, NH), slowness_index.reshape(1, NP),
      jnp.asarray(twiddle), jnp.asarray(table, dtype=BF16))
    return got.reshape(8, 64, 64)


def solution(mesh):
    placed = (P("offset", "freq"), P(None, "offset"), P(), P())
    return jax.shard_map(
        local, mesh=mesh, in_specs=placed, out_specs=P("offset", "freq", None), check_vma=False
    )
```

time: 59.3 us -> 55.8 us (0.941)
  local copies, waits for them, and re-layouts: 5.47 us -> 1.67 us
  Pallas kernels: 53.3 us -> 54 us
    unnamed x13 -> x1, local copies, waits for them, and re-layouts: 5.47 us -> 1.67 us
    pallas_call x1, Pallas kernels: 53.3 us -> 54 us  [local(): pl.pallas_call(kernel, out_shape=jax.ShapeDtypeStruct((8 * 64, 64), F32),...]
where the time goes in v3:
time: 55.8 us; the launch traced here: 55.7 us
  Pallas kernels  54 us (97%)
  local copies, waits for them, and re-layouts  1.67 us (3%)
    pallas_call x1, Pallas kernels, local(): pl.pallas_call(kernel, out_shape=jax.ShapeDtypeStruct((8 * 64, 64), F32),...  54 us
    unnamed x1, local copies, waits for them, and re-layouts  1.67 us

profile of v3, /device:TPU:1, one launch (start us, length us, event | category | flops | bytes accessed | tf_op | source)
XLA Modules:
  0.0 55.7 jit_solution(10556806698178209312)
XLA Ops:
  0.0 54.0 %radon.1 = f32[512,64]{1,0:T(8,128)} custom-call(bf16[1024,128]{1,0:T(8,128)(2,1)} %raw_hbm.1, s32[32,32]{1,0:T(8,128)} %slot_hbm.1, s32[1,1024]{1,0:T(1,128)} %bitcast.4, s32[1,256]{1,0:T(1,128)} %bitcast.5, f32[8,256]{1,0:T(8,128)} %constant.4.clone.twid_hbm, bf16[512,512]{1,0:T(8,128)(2,1)} %constant.5.clone.table_hbm), custom_call_target="tpu_custom_call" | custom-call | tf_op jit(solution)/shard_map/radon/pallas_call | solution.py:285
  54.0 1.7 %copy.8 = f32[8,64,64]{2,1,0:T(8,128)} copy(f32[8,64,64]{2,1,0:T(8,128)} %bitcast.3) | data formatting | bytes 262144

commit v4 on v3

--- a/solution.py
+++ b/solution.py
@@ -64,9 +64,12 @@
     return total
 
 
-def far_first(i, n):
-    half = n // 2
-    return half + ((i + 1) // 2) * (1 - 2 * (i % 2))
+def far_first(n):
+    return sorted(range(n), key=lambda d: -min(d, n - d))
+
+
+def wrap(value, n):
+    return jnp.where(value >= n, value - n, value)
 
 
 def kernel(raw_hbm, slot_hbm, offs_hbm, slow_hbm, twid_hbm, table_hbm, out,
@@ -77,13 +80,13 @@
     me_o = lax.axis_index("offset")
     me_x, me_z = me_o // NZ, me_o % NZ
 
-    def peer_k(i):
-        return (me_k + far_first(i, NK)) % NK
-
-    def peer_o(i):
-        dz = far_first(i // NX, NZ)
-        dx = far_first(i % NX, NX)
-        return ((me_x + dx) % NX) * NZ + (me_z + dz) % NZ
+    peers_k = [wrap(me_k + d, NK) for d in far_first(NK) if d]
+    peers_z = {d: wrap(me_z + d, NZ) for d in range(NZ)}
+    peers_x = {d: wrap(me_x + d, NX) * NZ for d in range(NX)}
+    peers_o = [
+        peers_x[dx] + peers_z[dz]
+        for dz in far_first(NZ) for dx in far_first(NX) if dx or dz
+    ]
 
     loads = [
         pltpu.make_async_copy(src, dst, load_sems.at[i])
@@ -95,48 +98,31 @@
         load.start()
     barrier = pltpu.get_barrier_semaphore()
 
-    def greet_k(i, c):
-        pl.semaphore_signal(barrier, inc=1, device_id=(peer_k(i), me_o), device_id_type=MESH)
-        return c
-
-    def greet_o(i, c):
-        pl.semaphore_signal(barrier, inc=1, device_id=(me_k, peer_o(i)), device_id_type=MESH)
-        return c
-
-    lax.fori_loop(0, NO - 1, greet_o, 0)
-    lax.fori_loop(0, NK - 1, greet_k, 0)
-
-    def copy_k(src, dst, ssem, rsem, there, here):
-        return pltpu.make_async_remote_copy(
-            src_ref=src.at[there], dst_ref=dst.at[here], send_sem=ssem.at[there],
-            recv_sem=rsem.at[here], device_id=(there, me_o), device_id_type=MESH)
-
-    def copy_o(src, dst, ssem, rsem, there, here):
-        return pltpu.make_async_remote_copy(
-            src_ref=src.at[there], dst_ref=dst.at[here], send_sem=ssem.at[there],
-            recv_sem=rsem.at[here], device_id=(me_k, there), device_id_type=MESH)
+    for there in peers_o:
+        pl.semaphore_signal(barrier, inc=1, device_id=(me_k, there), device_id_type=MESH)
+    for there in peers_k:
+        pl.semaphore_signal(barrier, inc=1, device_id=(there, me_o), device_id_type=MESH)
 
     class Exchange:
-        def __init__(self, over_freq, *refs):
-            self.make, self.count, self.peer, self.me = (
-                (copy_k, NK - 1, peer_k, me_k) if over_freq else (copy_o, NO - 1, peer_o, me_o))
-            self.refs = refs
-
-        def each(self, act):
-            def step(i, c):
-                act(self.peer(i))
-                return c
-            lax.fori_loop(0, self.count, step, 0)
+        def __init__(self, over_freq, src, dst, ssem, rsem):
+            self.peers, self.me = (peers_k, me_k) if over_freq else (peers_o, me_o)
+            self.over_freq, self.src, self.dst, self.ssem, self.rsem = over_freq, src, dst, ssem, rsem
 
         def start(self):
-            self.each(lambda there: self.make(*self.refs, there, self.me).start())
-            self.refs[1][self.me] = self.refs[0][self.me]
+            for there in self.peers:
+                pltpu.make_async_remote_copy(
+                    src_ref=self.src.at[there], dst_ref=self.dst.at[self.me], send_sem=self.ssem,
+                    recv_sem=self.rsem, device_id=(there, me_o) if self.over_freq else (me_k, there),
+                    device_id_type=MESH).start()
+            self.dst[self.me] = self.src[self.me]
 
         def arrive(self):
-            self.each(lambda there: self.make(*self.refs, there, there).wait_recv())
+            part = self.dst.at[pl.ds(0, len(self.peers))]
+            pltpu.make_async_copy(part, part, self.rsem).wait()
 
         def leave(self):
-            self.each(lambda there: self.make(*self.refs, there, self.me).wait_send())
+            part = self.src.at[pl.ds(0, len(self.peers))]
+            pltpu.make_async_copy(part, part, self.ssem).wait()
 
     def halves(over_freq, *refs):
         return [Exchange(over_freq, *(ref.at[h] for ref in refs)) for h in range(2)]
@@ -300,8 +286,8 @@
             pltpu.VMEM((2, 2 * NP, NH), BF16),
             pltpu.VMEM((NP, 128), F32),
             pltpu.VMEM((NO, 8, 128), BF16), pltpu.VMEM((NO, 8, 128), BF16),
-            dma((2, NK)), dma((2, NK)), dma((2, NK)), dma((2, NK)),
-            dma((2, NO)), dma((2, NO)), dma((NO,)), dma((NO,)), dma((6,)),
+            dma((2,)), dma((2,)), dma((2,)), dma((2,)),
+            dma((2,)), dma((2,)), dma(()), dma(()), dma((6,)),
         ],
         compiler_params=pltpu.CompilerParams(collective_id=0, has_side_effects=True),
         name="radon",

time: 55.8 us -> 47.5 us (0.85)
  Pallas kernels: 54 us -> 45.7 us
    pallas_call x1, Pallas kernels: 54 us -> 45.7 us  [local(): pl.pallas_call(kernel, out_shape=jax.ShapeDtypeStruct((8 * 64, 64), F32),...]
where the time goes in v4:
time: 47.5 us; the launch traced here: 47.3 us
  Pallas kernels  45.7 us (96%)
  local copies, waits for them, and re-layouts  1.67 us (4%)
    pallas_call x1, Pallas kernels, local(): pl.pallas_call(kernel, out_shape=jax.ShapeDtypeStruct((8 * 64, 64), F32),...  45.7 us
    unnamed x1, local copies, waits for them, and re-layouts  1.67 us

profile of v4, /device:TPU:1, one launch (start us, length us, event | category | flops | bytes accessed | tf_op | source)
XLA Modules:
  0.0 47.3 jit_solution(918304735189026502)
XLA Ops:
  0.0 45.7 %radon.1 = f32[512,64]{1,0:T(8,128)} custom-call(bf16[1024,128]{1,0:T(8,128)(2,1)} %raw_hbm.1, s32[32,32]{1,0:T(8,128)} %slot_hbm.1, s32[1,1024]{1,0:T(1,128)} %bitcast.4, s32[1,256]{1,0:T(1,128)} %bitcast.5, f32[8,256]{1,0:T(8,128)} %constant.4.clone.twid_hbm, bf16[512,512]{1,0:T(8,128)(2,1)} %constant.5.clone.table_hbm), custom_call_target="tpu_custom_call" | custom-call | tf_op jit(solution)/shard_map/radon/pallas_call | solution.py:271
  45.7 1.7 %copy.8 = f32[8,64,64]{2,1,0:T(8,128)} copy(f32[8,64,64]{2,1,0:T(8,128)} %bitcast.3) | data formatting | bytes 262144

commit v5 on v4

--- a/solution.py
+++ b/solution.py
@@ -74,13 +74,14 @@
 
 def kernel(raw_hbm, slot_hbm, offs_hbm, slow_hbm, twid_hbm, table_hbm, out,
            raw, slot, offs, slow, twid, table, send_a, recv_a, spec, send_c, recv_c, wide,
-           send_b, recv_b, columns, spectra, weights, curve, send_d, recv_d,
+           send_b, recv_b, places, weights, curve, sums, send_d, recv_d,
            ssem_a, rsem_a, ssem_b, rsem_b, ssem_c, rsem_c, ssem_d, rsem_d, load_sems):
     me_k = lax.axis_index("freq")
     me_o = lax.axis_index("offset")
     me_x, me_z = me_o // NZ, me_o % NZ
 
-    peers_k = [wrap(me_k + d, NK) for d in far_first(NK) if d]
+    turns_k = far_first(NK)
+    peers_k = [wrap(me_k + d, NK) for d in turns_k if d]
     peers_z = {d: wrap(me_z + d, NZ) for d in range(NZ)}
     peers_x = {d: wrap(me_x + d, NX) * NZ for d in range(NX)}
     peers_o = [
@@ -108,13 +109,19 @@
             self.peers, self.me = (peers_k, me_k) if over_freq else (peers_o, me_o)
             self.over_freq, self.src, self.dst, self.ssem, self.rsem = over_freq, src, dst, ssem, rsem
 
+        def send(self, there, slot):
+            pltpu.make_async_remote_copy(
+                src_ref=self.src.at[slot], dst_ref=self.dst.at[self.me], send_sem=self.ssem,
+                recv_sem=self.rsem, device_id=(there, me_o) if self.over_freq else (me_k, there),
+                device_id_type=MESH).start()
+
+        def keep(self, slot):
+            self.dst[self.me] = self.src[slot]
+
         def start(self):
             for there in self.peers:
-                pltpu.make_async_remote_copy(
-                    src_ref=self.src.at[there], dst_ref=self.dst.at[self.me], send_sem=self.ssem,
-                    recv_sem=self.rsem, device_id=(there, me_o) if self.over_freq else (me_k, there),
-                    device_id_type=MESH).start()
-            self.dst[self.me] = self.src[self.me]
+                self.send(there, there)
+            self.keep(self.me)
 
         def arrive(self):
             part = self.dst.at[pl.ds(0, len(self.peers))]
@@ -135,27 +142,56 @@
     loads[0].wait()
     loads[1].wait()
     row_ids = lax.broadcasted_iota(jnp.int32, (G, HB * G), 1)
-
-    def pick(h):
-        for part in range(2):
-            chosen = jnp.concatenate([
-                jnp.where(slot[:, 2 * kk + h:2 * kk + h + 1] == row_ids, 1.0, 0.0).astype(BF16)
-                for kk in range(8 * part, 8 * part + 8)
-            ], axis=0)
-            rows = jnp.dot(chosen, raw[...], preferred_element_type=F32).astype(BF16)
-            send_a[h, 8 * part:8 * part + 8] = rows.reshape(8, G, 128)
-
-    pick(0)
+    ahead = pltpu.roll(jnp.concatenate([slot[...]] * 4, axis=1), 4 * HB - 2 * me_k, 1)
+
+    def pick(h, part):
+        turns = turns_k[8 * part:8 * part + 8]
+        chosen = jnp.concatenate([
+            jnp.where(ahead[:, 2 * d + h:2 * d + h + 1] == row_ids, 1.0, 0.0).astype(BF16)
+            for d in turns
+        ], axis=0)
+        rows = jnp.dot(chosen, raw[...], preferred_element_type=F32).astype(BF16)
+        send_a[h, 8 * part:8 * part + 8] = rows.reshape(8, G, 128)
+
+    def post(h, part):
+        for i in range(8 * part, 8 * part + 8):
+            if turns_k[i]:
+                ex_a[h].send(peers_k[i], i)
+            else:
+                ex_a[h].keep(i)
+
+    pick(0, 0)
     pl.semaphore_wait(barrier, NO - 1 + NK - 1)
-    ex_a[0].start()
-    pick(1)
-    ex_a[1].start()
+    post(0, 0)
+    for h, part in [(0, 1), (1, 0), (1, 1)]:
+        pick(h, part)
+        post(h, part)
 
     loads[2].wait()
     loads[3].wait()
     for half in range(2):
         row = slow[:, 128 * half:128 * half + 128].astype(F32) * CURVATURE
         curve[128 * half:128 * half + 128, :] = jnp.transpose(jnp.broadcast_to(row, (128, 128)))
+    group = lax.broadcasted_iota(jnp.int32, (32, 128), 0)
+    lane = lax.broadcasted_iota(jnp.int32, (32, 128), 1)
+    eight = lax.broadcasted_iota(jnp.int32, (8, 128), 0)
+    lane8 = lax.broadcasted_iota(jnp.int32, (8, 128), 1)
+    grid = offs[...]
+    place = None
+    for size, digit in [(32.0, grid // 32), (1.0, grid % 32)]:
+        digit = digit.astype(F32).astype(BF16)
+        for m in range(4):
+            wanted = 32 * m + 2 * (group % NK) + group // NK
+            take = jnp.where(lane == wanted, 1.0, 0.0).astype(BF16)
+            some = lax.dot_general(take, digit, (((1,), (1,)), ((), ())), preferred_element_type=F32)
+            spread = jnp.where(lane8 % 32 == 4 * eight + m, size, 0.0).astype(BF16)
+            term = jnp.dot(some.astype(BF16), spread, preferred_element_type=F32)
+            place = term if place is None else place + term
+    for tile in range(NH // 128):
+        row = place[4 * tile:4 * tile + 1, :]
+        for i in range(1, 4):
+            row = jnp.where(lane[0:1] // 32 == i, place[4 * tile + i:4 * tile + i + 1, :], row)
+        places[:, 128 * tile:128 * tile + 128] = row
     first = 64 * me_k + 8 * me_z + me_x
     second = 64 * me_k + 8 * me_z + 7 - me_x
     rates = [(2 * f + 1).astype(F32) * (1.0 / (2 * NT)) for f in (first, second)]
@@ -166,7 +202,7 @@
         steep = curve[rows, :]
         for part in range(NH // 256):
             lanes = slice(256 * part, 256 * part + 256)
-            spread = jnp.concatenate([steep, steep], axis=1) * offs[:, lanes].astype(F32)
+            spread = jnp.concatenate([steep, steep], axis=1) * places[:, lanes]
             delay = jnp.sqrt(APEX_TIME * APEX_TIME + spread * spread) - APEX_TIME
             for f in range(2):
                 turns = delay * rates[f]
@@ -231,28 +267,34 @@
         ex_c[h].arrive()
         regroup(h)
         ex_b[h].start()
-    for h in range(2):
-        ex_b[h].arrive()
-        for kk in range(NK):
-            base = 2 * NO * kk + NO * h
-            columns[base:base + NO, :] = recv_b[h, kk].astype(F32)
-    for o in range(NO):
-        spectra[HB * o:HB * o + HB, :] = columns[pl.ds(o, HB, stride=NO), :].astype(BF16)
-
-    lane2 = lax.broadcasted_iota(jnp.int32, (64, 128), 1)
-    for block in range(NP // 64):
+
+    def merged(rows, h, side):
+        data = recv_b[h].reshape(NH // 2, 128)
+        lanes = slice(NH // 2 * h, NH // 2 * h + NH // 2)
+        both = [jnp.dot(weights[f, rows, lanes], data, preferred_element_type=F32) for f in range(2)]
+        return jnp.where(side, both[0], both[1])
+
+    side = lax.broadcasted_iota(jnp.int32, (64, 128), 1)
+    ex_b[0].arrive()
+    for block in range(2 * NP // 64):
         rows = slice(64 * block, 64 * block + 64)
-        low = slice(NP + 64 * block, NP + 64 * block + 64)
-        data = spectra[...]
-        cosine = [jnp.dot(weights[f, rows, :], data, preferred_element_type=F32) for f in range(2)]
-        sines = [jnp.dot(weights[f, low, :], data, preferred_element_type=F32) for f in range(2)]
-        ca = jnp.where(lane2 < 64, cosine[0], cosine[1])
-        sa = jnp.where(lane2 < 64, sines[0], sines[1])
-        swapped = jnp.where(lane2 % 64 < 32, -pltpu.roll(sa, 96, 1), pltpu.roll(sa, 32, 1))
+        sums[rows, :] = merged(rows, 0, side < 64)
+    ex_b[1].arrive()
+    for dx in far_first(NX):
+        start = peers_x[dx] * 8
+        rows = pl.ds(pl.multiple_of(start, 64), 64)
+        low = pl.ds(pl.multiple_of(start + NP, 64), 64)
+        ca = sums[rows, :] + merged(rows, 1, side < 64)
+        sa = sums[low, :] + merged(low, 1, side < 64)
+        swapped = jnp.where(side % 64 < 32, -pltpu.roll(sa, 96, 1), pltpu.roll(sa, 32, 1))
         panel = (ca + swapped) * (1.0 / math.sqrt(NH))
-        send_d[8 * block:8 * block + 8] = panel.reshape(8, 8, 128).astype(send_d.dtype)
-
-    ex_d.start()
+        send_d[pl.ds(peers_x[dx], 8)] = panel.reshape(8, 8, 128).astype(BF16)
+        for dz in far_first(NZ):
+            there = peers_x[dx] + peers_z[dz]
+            if dx or dz:
+                ex_d.send(there, there)
+            else:
+                ex_d.keep(there)
     ex_d.arrive()
     for o in range(NO):
         one = recv_d[o].astype(F32)
@@ -275,23 +317,23 @@
         out_specs=pl.BlockSpec(memory_space=pltpu.VMEM),
         scratch_shapes=[
             pltpu.VMEM((HB * G, 128), BF16), pltpu.VMEM((G, HB), jnp.int32),
-            pltpu.VMEM((1, NH), jnp.int32), pltpu.VMEM((1, NP), jnp.int32),
+            pltpu.VMEM((8, 128), jnp.int32), pltpu.VMEM((1, NP), jnp.int32),
             pltpu.VMEM((8, 256), F32), pltpu.VMEM((512, 512), BF16),
             pltpu.VMEM((2, NK, G, 128), BF16), pltpu.VMEM((2, NK, G, 128), BF16),
             pltpu.VMEM((256, 512), BF16),
             pltpu.VMEM((2, NO, NK, 128), BF16), pltpu.VMEM((2, NO, NK, 128), BF16),
             pltpu.VMEM((NO * NK, 128), F32),
             pltpu.VMEM((2, NK, NO, 128), BF16), pltpu.VMEM((2, NK, NO, 128), BF16),
-            pltpu.VMEM((NK * 2 * NO, 128), F32), pltpu.VMEM((NH, 128), BF16),
+            pltpu.VMEM((1, NH), F32),
             pltpu.VMEM((2, 2 * NP, NH), BF16),
-            pltpu.VMEM((NP, 128), F32),
+            pltpu.VMEM((NP, 128), F32), pltpu.VMEM((2 * NP, 128), F32),
             pltpu.VMEM((NO, 8, 128), BF16), pltpu.VMEM((NO, 8, 128), BF16),
             dma((2,)), dma((2,)), dma((2,)), dma((2,)),
             dma((2,)), dma((2,)), dma(()), dma(()), dma((6,)),
         ],
         compiler_params=pltpu.CompilerParams(collective_id=0, has_side_effects=True),
         name="radon",
-    )(raw_traces, trace_slot, offset_index.reshape(1, NH), slowness_index.reshape(1, NP),
+    )(raw_traces, trace_slot, offset_index.reshape(8, 128), slowness_index.reshape(1, NP),
       jnp.asarray(twiddle), jnp.asarray(table, dtype=BF16))
     return got.reshape(8, 64, 64)
 

time: 47.5 us -> 46.9 us (0.987)
  Pallas kernels: 45.7 us -> 45 us
    pallas_call x1, Pallas kernels: 45.7 us -> 45 us  [local(): pl.pallas_call(kernel, out_shape=jax.ShapeDtypeStruct((8 * 64, 64), F32),...]
where the time goes in v5:
time: 46.9 us; the launch traced here: 46.7 us
  Pallas kernels  45 us (96%)
  local copies, waits for them, and re-layouts  1.67 us (4%)
    pallas_call x1, Pallas kernels, local(): pl.pallas_call(kernel, out_shape=jax.ShapeDtypeStruct((8 * 64, 64), F32),...  45 us
    unnamed x1, local copies, waits for them, and re-layouts  1.67 us

profile of v5, /device:TPU:1, one launch (start us, length us, event | category | flops | bytes accessed | tf_op | source)
XLA Modules:
  0.0 46.7 jit_solution(312117276105408706)
XLA Ops:
  0.0 45.0 %radon.1 = f32[512,64]{1,0:T(8,128)} custom-call(bf16[1024,128]{1,0:T(8,128)(2,1)} %raw_hbm.1, s32[32,32]{1,0:T(8,128)} %slot_hbm.1, s32[8,128]{1,0:T(8,128)} %bitcast.4, s32[1,256]{1,0:T(1,128)} %bitcast.5, f32[8,256]{1,0:T(8,128)} %constant.4.clone.twid_hbm, bf16[512,512]{1,0:T(8,128)(2,1)} %constant.5.clone.table_hbm), custom_call_target="tpu_custom_call" | custom-call | tf_op jit(solution)/shard_map/radon/pallas_call | solution.py:313
  45.0 1.7 %copy.8 = f32[8,64,64]{2,1,0:T(8,128)} copy(f32[8,64,64]{2,1,0:T(8,128)} %bitcast.3) | data formatting | bytes 262144

commit v6 on v5

--- a/solution.py
+++ b/solution.py
@@ -140,16 +140,17 @@
     ex_d = Exchange(False, send_d, recv_d, ssem_d, rsem_d)
 
     loads[0].wait()
-    loads[1].wait()
     row_ids = lax.broadcasted_iota(jnp.int32, (G, HB * G), 1)
     ahead = pltpu.roll(jnp.concatenate([slot[...]] * 4, axis=1), 4 * HB - 2 * me_k, 1)
 
-    def pick(h, part):
+    def choose(h, part):
         turns = turns_k[8 * part:8 * part + 8]
-        chosen = jnp.concatenate([
+        return jnp.concatenate([
             jnp.where(ahead[:, 2 * d + h:2 * d + h + 1] == row_ids, 1.0, 0.0).astype(BF16)
             for d in turns
         ], axis=0)
+
+    def pick(h, part, chosen):
         rows = jnp.dot(chosen, raw[...], preferred_element_type=F32).astype(BF16)
         send_a[h, 8 * part:8 * part + 8] = rows.reshape(8, G, 128)
 
@@ -160,11 +161,13 @@
             else:
                 ex_a[h].keep(i)
 
-    pick(0, 0)
+    chosen = choose(0, 0)
+    loads[1].wait()
+    pick(0, 0, chosen)
     pl.semaphore_wait(barrier, NO - 1 + NK - 1)
     post(0, 0)
     for h, part in [(0, 1), (1, 0), (1, 1)]:
-        pick(h, part)
+        pick(h, part, choose(h, part))
         post(h, part)
 
     loads[2].wait()
@@ -221,32 +224,29 @@
     lane = lax.broadcasted_iota(jnp.int32, (128, 128), 1) // 32
 
     def transform(h):
-        x = [
-            jnp.concatenate([recv_a[h, 2 * d], recv_a[h, 2 * d + 1]], axis=1).astype(F32)
-            for d in range(8)
-        ]
-        less = [x[d] - x[8 - d] for d in range(1, 4)]
-        more = [x[d] + x[8 - d] for d in range(1, 4)]
-        for b in range(4):
-            m = 2 * b + 1
-            yr = x[0]
-            yi = x[4] * (-math.sin(math.pi * m / 2))
-            for d in range(1, 4):
-                yr = yr + less[d - 1] * math.cos(math.pi * d * m / 8)
-                yi = yi - more[d - 1] * math.sin(math.pi * d * m / 8)
-            tc = twid[b:b + 1, :]
-            ts = twid[4 + b:5 + b, :]
-            for side, value in enumerate([yr * tc + yi * ts, yi * tc - yr * ts]):
-                high = value.astype(BF16)
-                rest = (value - high.astype(F32)).astype(BF16)
-                lanes = slice(256 * side, 256 * side + 256)
-                spec[G * b:G * b + G, lanes] = high
-                spec[128 + G * b:128 + G * b + G, lanes] = rest
-        parts = []
-        for c in range(4):
-            both = lax.dot_general(table[128 * c:128 * c + 128, :], spec[...],
-                                   (((1,), (1,)), ((), ())), preferred_element_type=F32)
-            parts.append(both[:, 0:128] + both[:, 128:256])
+        for part in range(2):
+            x = [recv_a[h, 2 * d + part].astype(F32) for d in range(8)]
+            less = [x[d] - x[8 - d] for d in range(1, 4)]
+            more = [x[d] + x[8 - d] for d in range(1, 4)]
+            for b in range(4):
+                m = 2 * b + 1
+                yr = x[0]
+                yi = x[4] * (-math.sin(math.pi * m / 2))
+                for d in range(1, 4):
+                    yr = yr + less[d - 1] * math.cos(math.pi * d * m / 8)
+                    yi = yi - more[d - 1] * math.sin(math.pi * d * m / 8)
+                tc = twid[b:b + 1, 128 * part:128 * part + 128]
+                ts = twid[4 + b:5 + b, 128 * part:128 * part + 128]
+                for half, value in enumerate([yr * tc + yi * ts, yi * tc - yr * ts]):
+                    high = value.astype(BF16)
+                    rest = (value - high.astype(F32)).astype(BF16)
+                    lanes = slice(256 * half + 128 * part, 256 * half + 128 * part + 128)
+                    spec[G * b:G * b + G, lanes] = high
+                    spec[128 + G * b:128 + G * b + G, lanes] = rest
+        whole = lax.dot_general(table[...], spec[...], (((1,), (1,)), ((), ())),
+                                preferred_element_type=F32)
+        whole = whole[:, 0:128] + whole[:, 128:256]
+        parts = [whole[128 * c:128 * c + 128, :] for c in range(4)]
         for b in range(4):
             total = None
             for c in range(4):
@@ -312,7 +312,7 @@
     dma = pltpu.SemaphoreType.DMA
     got = pl.pallas_call(
         kernel,
-        out_shape=jax.ShapeDtypeStruct((8 * 64, 64), F32),
+        out_shape=pltpu.VMEM((8 * 64, 64), F32),
         in_specs=[pl.BlockSpec(memory_space=pltpu.HBM)] * 6,
         out_specs=pl.BlockSpec(memory_space=pltpu.VMEM),
         scratch_shapes=[
@@ -331,10 +331,11 @@
             dma((2,)), dma((2,)), dma((2,)), dma((2,)),
             dma((2,)), dma((2,)), dma(()), dma(()), dma((6,)),
         ],
-        compiler_params=pltpu.CompilerParams(collective_id=0, has_side_effects=True),
+        compiler_params=pltpu.CompilerParams(collective_id=0, has_side_effects=True, vmem_limit_bytes=16 * 1024 * 1024),
         name="radon",
-    )(raw_traces, trace_slot, offset_index.reshape(8, 128), slowness_index.reshape(1, NP),
-      jnp.asarray(twiddle), jnp.asarray(table, dtype=BF16))
+    )(*(pltpu.with_memory_space_constraint(v, pltpu.HBM) for v in (
+        raw_traces, trace_slot, offset_index.reshape(8, 128), slowness_index.reshape(1, NP),
+        jnp.asarray(twiddle), jnp.asarray(table, dtype=BF16))))
     return got.reshape(8, 64, 64)
 
 

time: 46.9 us -> 45.2 us (0.964)
  local copies, waits for them, and re-layouts: 1.67 us -> 0.71 us
  Pallas kernels: 45 us -> 44.3 us
    unnamed x1, local copies, waits for them, and re-layouts: 1.67 us -> 0.71 us
    pallas_call x1, Pallas kernels: 45 us -> 44.3 us  [local(): pl.pallas_call(kernel, out_shape=pltpu.VMEM((8 * 64, 64), F32), in_specs=...]
where the time goes in v6:
time: 45.2 us; the launch traced here: 45 us
  Pallas kernels  44.3 us (98%)
  local copies, waits for them, and re-layouts  0.71 us (2%)
    pallas_call x1, Pallas kernels, local(): pl.pallas_call(kernel, out_shape=pltpu.VMEM((8 * 64, 64), F32), in_specs=...  44.3 us

profile of v6, /device:TPU:1, one launch (start us, length us, event | category | flops | bytes accessed | tf_op | source)
XLA Modules:
  0.0 45.0 jit_solution(4024802829209336859)
XLA Ops:
  0.0 44.3 %radon.1 = f32[512,64]{1,0:T(8,128)S(1)} custom-call(bf16[1024,128]{1,0:T(8,128)(2,1)} %raw_hbm.1, s32[32,32]{1,0:T(8,128)} %slot_hbm.1, s32[8,128]{1,0:T(8,128)} %bitcast.4, s32[1,256]{1,0:T(1,128)} %bitcast.5, f32[8,256]{1,0:T(8,128)} %constant.4.clone.twid_hbm, bf16[512,512]{1,0:T(8,128)(2,1)} %constant.5.clone.table_hbm), custom_call_target="tpu_custom_call" | custom-call | tf_op jit(solution)/shard_map/radon/pallas_call | solution.py:313
  44.3 0.7 %copy.8 = f32[8,64,64]{2,1,0:T(8,128)} copy(f32[8,64,64]{2,1,0:T(8,128)S(1)} %bitcast.3) | data formatting | bytes 262144

commit v7 on v6

--- a/solution.py
+++ b/solution.py
@@ -75,7 +75,7 @@
 def kernel(raw_hbm, slot_hbm, offs_hbm, slow_hbm, twid_hbm, table_hbm, out,
            raw, slot, offs, slow, twid, table, send_a, recv_a, spec, send_c, recv_c, wide,
            send_b, recv_b, places, weights, curve, sums, send_d, recv_d,
-           ssem_a, rsem_a, ssem_b, rsem_b, ssem_c, rsem_c, ssem_d, rsem_d, load_sems):
+           ssem_a, rsem_a, ssem_b, rsem_b, ssem_c, rsem_c, ssem_d, rsem_d, load_sems, plane_sem):
     me_k = lax.axis_index("freq")
     me_o = lax.axis_index("offset")
     me_x, me_z = me_o // NZ, me_o % NZ
@@ -95,14 +95,18 @@
             (slot_hbm, slot), (raw_hbm, raw), (offs_hbm, offs), (slow_hbm, slow),
             (twid_hbm, twid), (table_hbm, table)])
     ]
-    for load in loads:
-        load.start()
     barrier = pltpu.get_barrier_semaphore()
-
-    for there in peers_o:
-        pl.semaphore_signal(barrier, inc=1, device_id=(me_k, there), device_id_type=MESH)
+    loads[0].start()
+    loads[1].start()
+
     for there in peers_k:
         pl.semaphore_signal(barrier, inc=1, device_id=(there, me_o), device_id_type=MESH)
+    line_z = [me_x * NZ + peers_z[d] for d in far_first(NZ) if d]
+    line_x = [peers_x[d] + me_z for d in far_first(NX) if d]
+    for there in line_z + line_x:
+        pl.semaphore_signal(barrier, inc=1, device_id=(me_k, there), device_id_type=MESH)
+    for load in loads[2:]:
+        load.start()
 
     class Exchange:
         def __init__(self, over_freq, src, dst, ssem, rsem):
@@ -164,8 +168,10 @@
     chosen = choose(0, 0)
     loads[1].wait()
     pick(0, 0, chosen)
-    pl.semaphore_wait(barrier, NO - 1 + NK - 1)
+    pl.semaphore_wait(barrier, NK - 1 + NZ - 1 + NX - 1)
     post(0, 0)
+    for there in line_x:
+        pl.semaphore_signal(plane_sem, inc=1, device_id=(me_k, there), device_id_type=MESH)
     for h, part in [(0, 1), (1, 0), (1, 1)]:
         pick(h, part, choose(h, part))
         post(h, part)
@@ -262,6 +268,8 @@
     for h in range(2):
         ex_a[h].arrive()
         transform(h)
+        if h == 0:
+            pl.semaphore_wait(plane_sem, NX - 1)
         ex_c[h].start()
     for h in range(2):
         ex_c[h].arrive()
@@ -329,7 +337,7 @@
             pltpu.VMEM((NP, 128), F32), pltpu.VMEM((2 * NP, 128), F32),
             pltpu.VMEM((NO, 8, 128), BF16), pltpu.VMEM((NO, 8, 128), BF16),
             dma((2,)), dma((2,)), dma((2,)), dma((2,)),
-            dma((2,)), dma((2,)), dma(()), dma(()), dma((6,)),
+            dma((2,)), dma((2,)), dma(()), dma(()), dma((6,)), pltpu.SemaphoreType.REGULAR,
         ],
         compiler_params=pltpu.CompilerParams(collective_id=0, has_side_effects=True, vmem_limit_bytes=16 * 1024 * 1024),
         name="radon",

time: 45.2 us -> 43.8 us (0.969)
  Pallas kernels: 44.3 us -> 43 us
    pallas_call x1, Pallas kernels: 44.3 us -> 43 us  [local(): pl.pallas_call(kernel, out_shape=pltpu.VMEM((8 * 64, 64), F32), in_specs=...]
where the time goes in v7:
time: 43.8 us; the launch traced here: 43.7 us
  Pallas kernels  43 us (98%)
  local copies, waits for them, and re-layouts  0.71 us (2%)
    pallas_call x1, Pallas kernels, local(): pl.pallas_call(kernel, out_shape=pltpu.VMEM((8 * 64, 64), F32), in_specs=...  43 us

profile of v7, /device:TPU:1, one launch (start us, length us, event | category | flops | bytes accessed | tf_op | source)
XLA Modules:
  0.0 43.7 jit_solution(12564841455974895230)
XLA Ops:
  0.0 43.0 %radon.1 = f32[512,64]{1,0:T(8,128)S(1)} custom-call(bf16[1024,128]{1,0:T(8,128)(2,1)} %raw_hbm.1, s32[32,32]{1,0:T(8,128)} %slot_hbm.1, s32[8,128]{1,0:T(8,128)} %bitcast.4, s32[1,256]{1,0:T(1,128)} %bitcast.5, f32[8,256]{1,0:T(8,128)} %constant.4.clone.twid_hbm, bf16[512,512]{1,0:T(8,128)(2,1)} %constant.5.clone.table_hbm), custom_call_target="tpu_custom_call" | custom-call | tf_op jit(solution)/shard_map/radon/pallas_call | solution.py:321
  43.0 0.7 %copy.8 = f32[8,64,64]{2,1,0:T(8,128)} copy(f32[8,64,64]{2,1,0:T(8,128)S(1)} %bitcast.3) | data formatting | bytes 262144

commit v8 on v7

--- a/solution.py
+++ b/solution.py
@@ -18,6 +18,7 @@
 NK = 16
 NO = 32
 NX = 4
+NY = 8
 NZ = 8
 APEX_TIME = 100.0
 CURVATURE = 0.0003
@@ -28,21 +29,26 @@
 
 def dft_tables():
     n = np.arange(256)[None, :]
-    row = np.arange(128)
-    a = (row % NK * NZ + row // NK)[:, None]
-    t0 = 2 * np.pi * ((a * n) % 256) / 256
-    t1 = 2 * np.pi * (((255 - a) * n) % 256) / 256
-    rows = [
-        np.concatenate([np.cos(t0), np.sin(t0)], 1),
-        np.concatenate([-np.sin(t0), np.cos(t0)], 1),
-        np.concatenate([np.cos(t1), np.sin(t1)], 1),
-        np.concatenate([np.sin(t1), -np.cos(t1)], 1),
-    ]
-    table = np.concatenate(rows, 0)
+    high = np.arange(64) // 8
+    low = np.arange(64) % 8
+    tables = []
+    for core in range(2):
+        same = 8 * (2 * low + core) + high
+        other = 8 * (2 * high + 1 - core) + low
+        a = np.concatenate([same, other])[:, None]
+        t0 = 2 * np.pi * ((a * n) % 256) / 256
+        t1 = 2 * np.pi * (((255 - a) * n) % 256) / 256
+        rows = [
+            np.concatenate([np.cos(t0), np.sin(t0)], 1),
+            np.concatenate([-np.sin(t0), np.cos(t0)], 1),
+            np.concatenate([np.cos(t1), np.sin(t1)], 1),
+            np.concatenate([np.sin(t1), -np.cos(t1)], 1),
+        ]
+        tables.append(np.concatenate(rows, 0))
     m = 2 * np.arange(4)[:, None] + 1
     turn = np.pi * (m * n) / 2048
     twiddle = np.concatenate([np.cos(turn), np.sin(turn)], 0) / math.sqrt(NT)
-    return table.astype(np.float32), twiddle.astype(np.float32)
+    return np.stack(tables).astype(np.float32), twiddle.astype(np.float32)
 
 
 def half_turn_fit(odd, terms):
@@ -73,12 +79,14 @@
 
 
 def kernel(raw_hbm, slot_hbm, offs_hbm, slow_hbm, twid_hbm, table_hbm, out,
-           raw, slot, offs, slow, twid, table, send_a, recv_a, spec, send_c, recv_c, wide,
-           send_b, recv_b, places, weights, curve, sums, send_d, recv_d,
-           ssem_a, rsem_a, ssem_b, rsem_b, ssem_c, rsem_c, ssem_d, rsem_d, load_sems, plane_sem):
+           raw, slot, offs, slow, twid, table, send_a, recv_a, spec, wide,
+           send_p, recv_p, send_r, recv_r, send_s, recv_s, send_t, recv_t, places, weights, curve, sums, send_d, recv_d,
+           ssems, rsems, load_sems, plane_sem):
     me_k = lax.axis_index("freq")
     me_o = lax.axis_index("offset")
     me_x, me_z = me_o // NZ, me_o % NZ
+    me_y = me_k // 2
+    me_c = me_k - 2 * me_y
 
     turns_k = far_first(NK)
     peers_k = [wrap(me_k + d, NK) for d in turns_k if d]
@@ -93,7 +101,7 @@
         pltpu.make_async_copy(src, dst, load_sems.at[i])
         for i, (src, dst) in enumerate([
             (slot_hbm, slot), (raw_hbm, raw), (offs_hbm, offs), (slow_hbm, slow),
-            (twid_hbm, twid), (table_hbm, table)])
+            (twid_hbm, twid), (table_hbm.at[me_c], table)])
     ]
     barrier = pltpu.get_barrier_semaphore()
     loads[0].start()
@@ -108,24 +116,30 @@
     for load in loads[2:]:
         load.start()
 
+    rings_y = [wrap(me_y + d, NY) for d in far_first(NY)]
+    to_k = [((there, me_o), there) for there in peers_k]
+    to_o = [((me_k, there), there) for there in peers_o]
+    to_same = [((2 * there + me_c, me_o), there) for there in rings_y[:-1]]
+    to_other = [((2 * there + 1 - me_c, me_o), there) for there in rings_y]
+    exchanges = []
+
     class Exchange:
-        def __init__(self, over_freq, src, dst, ssem, rsem):
-            self.peers, self.me = (peers_k, me_k) if over_freq else (peers_o, me_o)
-            self.over_freq, self.src, self.dst, self.ssem, self.rsem = over_freq, src, dst, ssem, rsem
-
-        def send(self, there, slot):
+        def __init__(self, src, dst, peers, me):
+            self.src, self.dst, self.peers, self.me = src, dst, peers, me
+            self.ssem, self.rsem = ssems.at[len(exchanges)], rsems.at[len(exchanges)]
+            exchanges.append(self)
+
+        def send(self, device, slot):
             pltpu.make_async_remote_copy(
                 src_ref=self.src.at[slot], dst_ref=self.dst.at[self.me], send_sem=self.ssem,
-                recv_sem=self.rsem, device_id=(there, me_o) if self.over_freq else (me_k, there),
-                device_id_type=MESH).start()
+                recv_sem=self.rsem, device_id=device, device_id_type=MESH).start()
 
         def keep(self, slot):
             self.dst[self.me] = self.src[slot]
 
         def start(self):
-            for there in self.peers:
-                self.send(there, there)
-            self.keep(self.me)
+            for device, slot in self.peers:
+                self.send(device, slot)
 
         def arrive(self):
             part = self.dst.at[pl.ds(0, len(self.peers))]
@@ -135,13 +149,15 @@
             part = self.src.at[pl.ds(0, len(self.peers))]
             pltpu.make_async_copy(part, part, self.ssem).wait()
 
-    def halves(over_freq, *refs):
-        return [Exchange(over_freq, *(ref.at[h] for ref in refs)) for h in range(2)]
-
-    ex_a = halves(True, send_a, recv_a, ssem_a, rsem_a)
-    ex_b = halves(True, send_b, recv_b, ssem_b, rsem_b)
-    ex_c = halves(False, send_c, recv_c, ssem_c, rsem_c)
-    ex_d = Exchange(False, send_d, recv_d, ssem_d, rsem_d)
+    def halves(src, dst, peers, me):
+        return [Exchange(src.at[h], dst.at[h], peers, me) for h in range(2)]
+
+    ex_a = halves(send_a, recv_a, to_k, me_k)
+    ex_p = halves(send_p, recv_p, to_o, me_o)
+    ex_s = halves(send_s, recv_s, to_same, me_y)
+    ex_r = halves(send_r, recv_r, to_other, me_y)
+    ex_t = halves(send_t, recv_t, to_o, me_o)
+    ex_d = Exchange(send_d, recv_d, to_o, me_o)
 
     loads[0].wait()
     row_ids = lax.broadcasted_iota(jnp.int32, (G, HB * G), 1)
@@ -161,7 +177,7 @@
     def post(h, part):
         for i in range(8 * part, 8 * part + 8):
             if turns_k[i]:
-                ex_a[h].send(peers_k[i], i)
+                ex_a[h].send((peers_k[i], me_o), i)
             else:
                 ex_a[h].keep(i)
 
@@ -181,26 +197,38 @@
     for half in range(2):
         row = slow[:, 128 * half:128 * half + 128].astype(F32) * CURVATURE
         curve[128 * half:128 * half + 128, :] = jnp.transpose(jnp.broadcast_to(row, (128, 128)))
-    group = lax.broadcasted_iota(jnp.int32, (32, 128), 0)
-    lane = lax.broadcasted_iota(jnp.int32, (32, 128), 1)
+    group = lax.broadcasted_iota(jnp.int32, (16, 128), 0)
+    lane = lax.broadcasted_iota(jnp.int32, (16, 128), 1)
     eight = lax.broadcasted_iota(jnp.int32, (8, 128), 0)
     lane8 = lax.broadcasted_iota(jnp.int32, (8, 128), 1)
+    deep = lax.broadcasted_iota(jnp.int32, (128, 128), 0)
+    lane128 = lax.broadcasted_iota(jnp.int32, (128, 128), 1)
     grid = offs[...]
+    digits = [(32.0, grid // 32), (1.0, grid % 32)]
+    digits = [(size, digit.astype(F32).astype(BF16)) for size, digit in digits]
     place = None
-    for size, digit in [(32.0, grid // 32), (1.0, grid % 32)]:
-        digit = digit.astype(F32).astype(BF16)
+    for size, digit in digits:
         for m in range(4):
-            wanted = 32 * m + 2 * (group % NK) + group // NK
+            wanted = 32 * m + 2 * (2 * (group % NY) + me_c) + group // NY
             take = jnp.where(lane == wanted, 1.0, 0.0).astype(BF16)
             some = lax.dot_general(take, digit, (((1,), (1,)), ((), ())), preferred_element_type=F32)
             spread = jnp.where(lane8 % 32 == 4 * eight + m, size, 0.0).astype(BF16)
             term = jnp.dot(some.astype(BF16), spread, preferred_element_type=F32)
             place = term if place is None else place + term
-    for tile in range(NH // 128):
-        row = place[4 * tile:4 * tile + 1, :]
-        for i in range(1, 4):
-            row = jnp.where(lane[0:1] // 32 == i, place[4 * tile + i:4 * tile + i + 1, :], row)
-        places[:, 128 * tile:128 * tile + 128] = row
+    for h in range(2):
+        wanted = (lane128 // 8 % 4) * 32 + 2 * (2 * (lane128 % 8) + 1 - me_c) + h
+        other = None
+        for size, digit in digits:
+            take = jnp.where(deep == wanted, size, 0.0).astype(BF16)
+            term = jnp.dot(digit, take, preferred_element_type=F32)
+            other = term if other is None else other + term
+        for source, base, start in [(place, NY * h, 512 * h), (other, 0, 512 * h + 256)]:
+            for tile in range(2):
+                at = base + 4 * tile
+                row = source[at:at + 1, :]
+                for i in range(1, 4):
+                    row = jnp.where(lane[0:1] // 32 == i, source[at + i:at + i + 1, :], row)
+                places[:, start + 128 * tile:start + 128 * tile + 128] = row
     first = 64 * me_k + 8 * me_z + me_x
     second = 64 * me_k + 8 * me_z + 7 - me_x
     rates = [(2 * f + 1).astype(F32) * (1.0 / (2 * NT)) for f in (first, second)]
@@ -253,41 +281,61 @@
                                 preferred_element_type=F32)
         whole = whole[:, 0:128] + whole[:, 128:256]
         parts = [whole[128 * c:128 * c + 128, :] for c in range(4)]
+        bottoms = []
         for b in range(4):
             total = None
             for c in range(4):
                 moved = parts[c] if c == b else pltpu.roll(parts[c], (c - b) * 32 % 128, 1)
                 total = moved if c == 0 else jnp.where(lane == c, moved, total)
-            send_c[h, 8 * b:8 * b + 8] = total.reshape(NZ, NK, 128).astype(BF16)
-
-    def regroup(h):
-        wide[...] = recv_c[h].astype(F32).reshape(NO * NK, 128)
-        for kk in range(NK):
-            send_b[h, kk] = wide[pl.ds(kk, NO, stride=NK), :].astype(BF16)
+            send_p[h, 8 * b:8 * b + 8] = total[0:64].reshape(NZ, NY, 128).astype(BF16)
+            bottoms.append(total[64:128].reshape(NY, NZ, 128))
+        for t in range(2):
+            pair = jnp.concatenate(bottoms[2 * t:2 * t + 2], axis=1).astype(BF16)
+            send_r[h, :, 16 * t:16 * t + 16, :] = pair
+
+    def turn_p(h):
+        wide[...] = recv_p[h].astype(F32).reshape(NO * NY, 128)
+        for y in range(NY):
+            send_s[h, y] = wide[pl.ds(y, NO, stride=NY), :].astype(BF16)
+
+    def turn_r(h):
+        wide[...] = recv_r[h].astype(F32).reshape(NO * NY, 128)
+        for o in range(NO):
+            send_t[h, o] = wide[pl.ds(o, NY, stride=NO), :].astype(BF16)
 
     for h in range(2):
         ex_a[h].arrive()
         transform(h)
         if h == 0:
             pl.semaphore_wait(plane_sem, NX - 1)
-        ex_c[h].start()
+        ex_p[h].start()
+        ex_r[h].start()
+        ex_p[h].keep(me_o)
     for h in range(2):
-        ex_c[h].arrive()
-        regroup(h)
-        ex_b[h].start()
+        ex_r[h].arrive()
+        turn_r(h)
+        ex_t[h].start()
+        ex_t[h].keep(me_o)
+        ex_p[h].arrive()
+        turn_p(h)
+        ex_s[h].start()
+        ex_s[h].keep(me_y)
 
     def merged(rows, h, side):
-        data = recv_b[h].reshape(NH // 2, 128)
+        data = jnp.concatenate(
+            [recv_s[h].reshape(NH // 4, 128), recv_t[h].astype(F32).reshape(NH // 4, 128).astype(BF16)])
         lanes = slice(NH // 2 * h, NH // 2 * h + NH // 2)
         both = [jnp.dot(weights[f, rows, lanes], data, preferred_element_type=F32) for f in range(2)]
         return jnp.where(side, both[0], both[1])
 
     side = lax.broadcasted_iota(jnp.int32, (64, 128), 1)
-    ex_b[0].arrive()
+    ex_s[0].arrive()
+    ex_t[0].arrive()
     for block in range(2 * NP // 64):
         rows = slice(64 * block, 64 * block + 64)
         sums[rows, :] = merged(rows, 0, side < 64)
-    ex_b[1].arrive()
+    ex_s[1].arrive()
+    ex_t[1].arrive()
     for dx in far_first(NX):
         start = peers_x[dx] * 8
         rows = pl.ds(pl.multiple_of(start, 64), 64)
@@ -300,7 +348,7 @@
         for dz in far_first(NZ):
             there = peers_x[dx] + peers_z[dz]
             if dx or dz:
-                ex_d.send(there, there)
+                ex_d.send((me_k, there), there)
             else:
                 ex_d.keep(there)
     ex_d.arrive()
@@ -311,7 +359,7 @@
         out[pl.ds(f0, 8, stride=64), :] = one[:, 0:64]
         out[pl.ds(f1, 8, stride=64), :] = one[:, 64:128]
 
-    for ex in ex_a + ex_b + ex_c + [ex_d]:
+    for ex in exchanges:
         ex.leave()
 
 
@@ -329,15 +377,16 @@
             pltpu.VMEM((8, 256), F32), pltpu.VMEM((512, 512), BF16),
             pltpu.VMEM((2, NK, G, 128), BF16), pltpu.VMEM((2, NK, G, 128), BF16),
             pltpu.VMEM((256, 512), BF16),
-            pltpu.VMEM((2, NO, NK, 128), BF16), pltpu.VMEM((2, NO, NK, 128), BF16),
-            pltpu.VMEM((NO * NK, 128), F32),
-            pltpu.VMEM((2, NK, NO, 128), BF16), pltpu.VMEM((2, NK, NO, 128), BF16),
+            pltpu.VMEM((NO * NY, 128), F32),
+            pltpu.VMEM((2, NO, NY, 128), BF16), pltpu.VMEM((2, NO, NY, 128), BF16),
+            pltpu.VMEM((2, NY, NO, 128), BF16), pltpu.VMEM((2, NY, NO, 128), BF16),
+            pltpu.VMEM((2, NY, NO, 128), BF16), pltpu.VMEM((2, NY, NO, 128), BF16),
+            pltpu.VMEM((2, NO, NY, 128), BF16), pltpu.VMEM((2, NO, NY, 128), BF16),
             pltpu.VMEM((1, NH), F32),
             pltpu.VMEM((2, 2 * NP, NH), BF16),
             pltpu.VMEM((NP, 128), F32), pltpu.VMEM((2 * NP, 128), F32),
             pltpu.VMEM((NO, 8, 128), BF16), pltpu.VMEM((NO, 8, 128), BF16),
-            dma((2,)), dma((2,)), dma((2,)), dma((2,)),
-            dma((2,)), dma((2,)), dma(()), dma(()), dma((6,)), pltpu.SemaphoreType.REGULAR,
+            dma((11,)), dma((11,)), dma((6,)), pltpu.SemaphoreType.REGULAR,
         ],
         compiler_params=pltpu.CompilerParams(collective_id=0, has_side_effects=True, vmem_limit_bytes=16 * 1024 * 1024),
         name="radon",

time: 43.8 us -> 40.5 us (0.925)
  Pallas kernels: 43 us -> 39.6 us
    pallas_call x1, Pallas kernels: 43 us -> 39.6 us  [local(): pl.pallas_call(kernel, out_shape=pltpu.VMEM((8 * 64, 64), F32), in_specs=...]
where the time goes in v8:
time: 40.5 us; the launch traced here: 40.3 us
  Pallas kernels  39.6 us (98%)
  local copies, waits for them, and re-layouts  0.71 us (2%)
    pallas_call x1, Pallas kernels, local(): pl.pallas_call(kernel, out_shape=pltpu.VMEM((8 * 64, 64), F32), in_specs=...  39.6 us

profile of v8, /device:TPU:1, one launch (start us, length us, event | category | flops | bytes accessed | tf_op | source)
XLA Modules:
  0.0 40.3 jit_solution(2462818987322957579)
XLA Ops:
  0.0 39.6 %radon.1 = f32[512,64]{1,0:T(8,128)S(1)} custom-call(bf16[1024,128]{1,0:T(8,128)(2,1)} %raw_hbm.1, s32[32,32]{1,0:T(8,128)} %slot_hbm.1, s32[8,128]{1,0:T(8,128)} %bitcast.4, s32[1,256]{1,0:T(1,128)} %bitcast.5, f32[8,256]{1,0:T(8,128)} %constant.4.clone.twid_hbm, bf16[2,512,512]{2,1,0:T(8,128)(2,1)} %constant.5.clone.table_hbm), custom_call_target="tpu_custom_call" | custom-call | tf_op jit(solution)/shard_map/radon/pallas_call | solution.py:369
  39.6 0.7 %copy.8 = f32[8,64,64]{2,1,0:T(8,128)} copy(f32[8,64,64]{2,1,0:T(8,128)S(1)} %bitcast.3) | data formatting | bytes 262144

commit v9 on v8

--- a/solution.py
+++ b/solution.py
@@ -80,7 +80,7 @@
 
 def kernel(raw_hbm, slot_hbm, offs_hbm, slow_hbm, twid_hbm, table_hbm, out,
            raw, slot, offs, slow, twid, table, send_a, recv_a, spec, wide,
-           send_p, recv_p, send_r, recv_r, send_s, recv_s, send_t, recv_t, places, weights, curve, sums, send_d, recv_d,
+           send_p, recv_p, send_r, recv_r, send_s, recv_s, send_t, recv_t, places, weights, spectra, curve, sums, send_d, recv_d,
            ssems, rsems, load_sems, plane_sem):
     me_k = lax.axis_index("freq")
     me_o = lax.axis_index("offset")
@@ -234,9 +234,10 @@
     rates = [(2 * f + 1).astype(F32) * (1.0 / (2 * NT)) for f in (first, second)]
 
     def weigh(block, c):
-        rows = pl.ds(pl.multiple_of(block * 16, 16), 16)
-        low = pl.ds(pl.multiple_of(block * 16 + NP, 16), 16)
-        steep = curve[rows, :]
+        steep = curve[pl.ds(pl.multiple_of(block * 16, 16), 16), :]
+        base = block // 4 * 128 + block % 4 * 16
+        rows = pl.ds(pl.multiple_of(base, 16), 16)
+        low = pl.ds(pl.multiple_of(base + 64, 16), 16)
         for part in range(NH // 256):
             lanes = slice(256 * part, 256 * part + 256)
             spread = jnp.concatenate([steep, steep], axis=1) * places[:, lanes]
@@ -247,8 +248,10 @@
                 r2 = r * r
                 s = horner(r2, SIN_FIT) * r
                 q = horner(r2, COS_FIT)
-                weights[f, rows, lanes] = (1.0 - 2.0 * (s * s)).astype(BF16)
-                weights[f, low, lanes] = (2.0 * (s * q)).astype(BF16)
+                start = part // 2 * NH + f * (NH // 2) + part % 2 * 256
+                into = slice(start, start + 256)
+                weights[rows, into] = (1.0 - 2.0 * (s * s)).astype(BF16)
+                weights[low, into] = (2.0 * (s * q)).astype(BF16)
         return c
 
     lax.fori_loop(0, NP // 16, weigh, 0)
@@ -308,8 +311,8 @@
         transform(h)
         if h == 0:
             pl.semaphore_wait(plane_sem, NX - 1)
+        ex_r[h].start()
         ex_p[h].start()
-        ex_r[h].start()
         ex_p[h].keep(me_o)
     for h in range(2):
         ex_r[h].arrive()
@@ -321,27 +324,32 @@
         ex_s[h].start()
         ex_s[h].keep(me_y)
 
-    def merged(rows, h, side):
-        data = jnp.concatenate(
-            [recv_s[h].reshape(NH // 4, 128), recv_t[h].astype(F32).reshape(NH // 4, 128).astype(BF16)])
-        lanes = slice(NH // 2 * h, NH // 2 * h + NH // 2)
-        both = [jnp.dot(weights[f, rows, lanes], data, preferred_element_type=F32) for f in range(2)]
-        return jnp.where(side, both[0], both[1])
-
+    def collect(h):
+        for start, rows in [(0, recv_s[h].reshape(NH // 4, 128).astype(F32)),
+                            (NH // 4, recv_t[h].astype(F32).reshape(NH // 4, 128))]:
+            for f in range(2):
+                at = start + f * (NH // 2)
+                kept = (deep2 < 64) if f == 0 else (deep2 >= 64)
+                spectra[at:at + NH // 4, :] = jnp.where(kept, rows, 0.0).astype(BF16)
+
+    def merged(rows, h):
+        return jnp.dot(weights[rows, NH * h:NH * h + NH], spectra[...], preferred_element_type=F32)
+
+    deep2 = lax.broadcasted_iota(jnp.int32, (NH // 4, 128), 1)
     side = lax.broadcasted_iota(jnp.int32, (64, 128), 1)
     ex_s[0].arrive()
     ex_t[0].arrive()
-    for block in range(2 * NP // 64):
-        rows = slice(64 * block, 64 * block + 64)
-        sums[rows, :] = merged(rows, 0, side < 64)
+    collect(0)
+    for block in range(2):
+        rows = slice(NP * block, NP * block + NP)
+        sums[rows, :] = merged(rows, 0)
     ex_s[1].arrive()
     ex_t[1].arrive()
+    collect(1)
     for dx in far_first(NX):
-        start = peers_x[dx] * 8
-        rows = pl.ds(pl.multiple_of(start, 64), 64)
-        low = pl.ds(pl.multiple_of(start + NP, 64), 64)
-        ca = sums[rows, :] + merged(rows, 1, side < 64)
-        sa = sums[low, :] + merged(low, 1, side < 64)
+        rows = pl.ds(pl.multiple_of(peers_x[dx] * 16, 128), 128)
+        both = sums[rows, :] + merged(rows, 1)
+        ca, sa = both[0:64], both[64:128]
         swapped = jnp.where(side % 64 < 32, -pltpu.roll(sa, 96, 1), pltpu.roll(sa, 32, 1))
         panel = (ca + swapped) * (1.0 / math.sqrt(NH))
         send_d[pl.ds(peers_x[dx], 8)] = panel.reshape(8, 8, 128).astype(BF16)
@@ -383,7 +391,7 @@
             pltpu.VMEM((2, NY, NO, 128), BF16), pltpu.VMEM((2, NY, NO, 128), BF16),
             pltpu.VMEM((2, NO, NY, 128), BF16), pltpu.VMEM((2, NO, NY, 128), BF16),
             pltpu.VMEM((1, NH), F32),
-            pltpu.VMEM((2, 2 * NP, NH), BF16),
+            pltpu.VMEM((2 * NP, 2 * NH), BF16), pltpu.VMEM((NH, 128), BF16),
             pltpu.VMEM((NP, 128), F32), pltpu.VMEM((2 * NP, 128), F32),
             pltpu.VMEM((NO, 8, 128), BF16), pltpu.VMEM((NO, 8, 128), BF16),
             dma((11,)), dma((11,)), dma((6,)), pltpu.SemaphoreType.REGULAR,

time: 40.5 us -> 40.4 us (level)
  no operation moved by 1% of the time
where the time goes in v9:
time: 40.4 us; the launch traced here: 40.2 us
  Pallas kernels  39.5 us (98%)
  local copies, waits for them, and re-layouts  0.71 us (2%)
    pallas_call x1, Pallas kernels, local(): pl.pallas_call(kernel, out_shape=pltpu.VMEM((8 * 64, 64), F32), in_specs=...  39.5 us

profile of v9, /device:TPU:1, one launch (start us, length us, event | category | flops | bytes accessed | tf_op | source)
XLA Modules:
  0.0 40.2 jit_solution(7261916078461704865)
XLA Ops:
  0.0 39.5 %radon.1 = f32[512,64]{1,0:T(8,128)S(1)} custom-call(bf16[1024,128]{1,0:T(8,128)(2,1)} %raw_hbm.1, s32[32,32]{1,0:T(8,128)} %slot_hbm.1, s32[8,128]{1,0:T(8,128)} %bitcast.4, s32[1,256]{1,0:T(1,128)} %bitcast.5, f32[8,256]{1,0:T(8,128)} %constant.4.clone.twid_hbm, bf16[2,512,512]{2,1,0:T(8,128)(2,1)} %constant.5.clone.table_hbm), custom_call_target="tpu_custom_call" | custom-call | tf_op jit(solution)/shard_map/radon/pallas_call | solution.py:377
  39.5 0.7 %copy.8 = f32[8,64,64]{2,1,0:T(8,128)} copy(f32[8,64,64]{2,1,0:T(8,128)S(1)} %bitcast.3) | data formatting | bytes 262144

commit v10 on v9

--- a/solution.py
+++ b/solution.py
@@ -346,19 +346,16 @@
     ex_s[1].arrive()
     ex_t[1].arrive()
     collect(1)
-    for dx in far_first(NX):
-        rows = pl.ds(pl.multiple_of(peers_x[dx] * 16, 128), 128)
+    for block in range(4):
+        rows = slice(128 * block, 128 * block + 128)
         both = sums[rows, :] + merged(rows, 1)
         ca, sa = both[0:64], both[64:128]
         swapped = jnp.where(side % 64 < 32, -pltpu.roll(sa, 96, 1), pltpu.roll(sa, 32, 1))
         panel = (ca + swapped) * (1.0 / math.sqrt(NH))
-        send_d[pl.ds(peers_x[dx], 8)] = panel.reshape(8, 8, 128).astype(BF16)
-        for dz in far_first(NZ):
-            there = peers_x[dx] + peers_z[dz]
-            if dx or dz:
-                ex_d.send((me_k, there), there)
-            else:
-                ex_d.keep(there)
+        send_d[8 * block:8 * block + 8] = panel.reshape(8, 8, 128).astype(BF16)
+    for device, slot in to_o:
+        ex_d.send(device, slot)
+    ex_d.keep(me_o)
     ex_d.arrive()
     for o in range(NO):
         one = recv_d[o].astype(F32)

time: 40.4 us -> 40.1 us (level)
  no operation moved by 1% of the time
where the time goes in v10:
time: 40.1 us; the launch traced here: 39.9 us
  Pallas kernels  39.2 us (98%)
  local copies, waits for them, and re-layouts  0.71 us (2%)
    pallas_call x1, Pallas kernels, local(): pl.pallas_call(kernel, out_shape=pltpu.VMEM((8 * 64, 64), F32), in_specs=...  39.2 us

profile of v10, /device:TPU:1, one launch (start us, length us, event | category | flops | bytes accessed | tf_op | source)
XLA Modules:
  0.0 39.9 jit_solution(2829958504818621125)
XLA Ops:
  0.0 39.2 %radon.1 = f32[512,64]{1,0:T(8,128)S(1)} custom-call(bf16[1024,128]{1,0:T(8,128)(2,1)} %raw_hbm.1, s32[32,32]{1,0:T(8,128)} %slot_hbm.1, s32[8,128]{1,0:T(8,128)} %bitcast.4, s32[1,256]{1,0:T(1,128)} %bitcast.5, f32[8,256]{1,0:T(8,128)} %constant.4.clone.twid_hbm, bf16[2,512,512]{2,1,0:T(8,128)(2,1)} %constant.5.clone.table_hbm), custom_call_target="tpu_custom_call" | custom-call | tf_op jit(solution)/shard_map/radon/pallas_call | solution.py:374
  39.2 0.7 %copy.8 = f32[8,64,64]{2,1,0:T(8,128)} copy(f32[8,64,64]{2,1,0:T(8,128)S(1)} %bitcast.3) | data formatting | bytes 262144

commit v11 on v10

--- a/solution.py
+++ b/solution.py
@@ -92,10 +92,10 @@
     peers_k = [wrap(me_k + d, NK) for d in turns_k if d]
     peers_z = {d: wrap(me_z + d, NZ) for d in range(NZ)}
     peers_x = {d: wrap(me_x + d, NX) * NZ for d in range(NX)}
-    peers_o = [
-        peers_x[dx] + peers_z[dz]
-        for dz in far_first(NZ) for dx in far_first(NX) if dx or dz
-    ]
+    hops = sorted(
+        [(dx, dz) for dz in far_first(NZ) for dx in far_first(NX) if dx or dz],
+        key=lambda d: -min(d[0], NX - d[0]) - min(d[1], NZ - d[1]))
+    peers_o = [peers_x[dx] + peers_z[dz] for dx, dz in hops]
 
     loads = [
         pltpu.make_async_copy(src, dst, load_sems.at[i])

time: 40.1 us -> 40.1 us (level)
  no operation moved by 1% of the time
where the time goes in v11:
time: 40.1 us; the launch traced here: 39.9 us
  Pallas kernels  39.2 us (98%)
  local copies, waits for them, and re-layouts  0.71 us (2%)
    pallas_call x1, Pallas kernels, local(): pl.pallas_call(kernel, out_shape=pltpu.VMEM((8 * 64, 64), F32), in_specs=...  39.2 us

profile of v11, /device:TPU:1, one launch (start us, length us, event | category | flops | bytes accessed | tf_op | source)
XLA Modules:
  0.0 39.9 jit_solution(5036014353645747426)
XLA Ops:
  0.0 39.2 %radon.1 = f32[512,64]{1,0:T(8,128)S(1)} custom-call(bf16[1024,128]{1,0:T(8,128)(2,1)} %raw_hbm.1, s32[32,32]{1,0:T(8,128)} %slot_hbm.1, s32[8,128]{1,0:T(8,128)} %bitcast.4, s32[1,256]{1,0:T(1,128)} %bitcast.5, f32[8,256]{1,0:T(8,128)} %constant.4.clone.twid_hbm, bf16[2,512,512]{2,1,0:T(8,128)(2,1)} %constant.5.clone.table_hbm), custom_call_target="tpu_custom_call" | custom-call | tf_op jit(solution)/shard_map/radon/pallas_call | solution.py:374
  39.2 0.7 %copy.8 = f32[8,64,64]{2,1,0:T(8,128)} copy(f32[8,64,64]{2,1,0:T(8,128)S(1)} %bitcast.3) | data formatting | bytes 262144
